TPU v7x, 32 devices: a whole 2x2x4 slice. The times are simulated.
32 devices in a mesh: avg: 4 (over x, core), space: 8 (over z, y).
Axes of the slice: x: 2, y: 2, z: 4, core: 2. Of those that a mesh axis runs over, the one named last changes fastest.
Arguments:
- spectral_state: float32 [3, 2, 1024, 1024], P(None, None, 'space', 'avg'), may hold values from -6 to 6
- phase_index: int32 [4], P('avg'), may hold values from 0 to 63
- weight_count: int32 [4], P('avg'), may hold values from 1 to 7
Outputs:
- advanced: float32 [3, 2, 1024, 1024], P(None, None, 'space', 'avg')
All inputs are finite; a program needn't handle non-finite values.
Results may differ from a plain program's by a relative error of at most 0.015.
Values may be sent and summed in bfloat16 or wider, within the bound.
A program may use at most 64 MiB of HBM per device.

v0:
```python
import jax
import jax.numpy as jnp
import ml_dtypes
import numpy as np
from jax import lax
from jax.sharding import PartitionSpec as P

coriolis = 1.0
wave_speed = 6.0
phase_step = 0.25
time_step = 2.0
weight_scale = 4.0


def wave_of(positions, length):
    shifted = (positions + length // 2) % length - length // 2
    return shifted.astype(jnp.float32) * (2.0 / length)


def circle(products, length):
    angles = (products % length) * (2.0 * np.pi / length)
    return np.cos(angles).astype(np.float32), np.sin(angles).astype(np.float32)


def slot_base(slot, slots, half):
    return np.where(slot < slots // 2, 2 * half * slot, 2 * half * (slots - 1 - slot) + half)


def packed_table(length, slots):
    half = length // (2 * slots)
    rows = slot_base(np.arange(slots), slots, half)[:, None] + np.arange(half)
    cosine, sine = circle(rows[:, :, None] * np.arange(length), length)
    packed = np.stack([cosine, -sine], axis=1)
    packed[0, 1, 0] = circle(length // 2 * np.arange(length), length)[0]
    return packed.astype(ml_dtypes.bfloat16)


def turned(first, second):
    (c, s), (d, t) = first, second
    return c * d - s * t, s * d + c * t


def column_tables(length, width, groups, order):
    fine = 1
    while fine * fine < width:
        fine *= 2
    y = np.arange(length)
    low = circle(np.arange(fine)[:, None] * y, length)
    high = circle(fine * np.arange(width // fine)[:, None] * y, length)
    block = circle(width * np.arange(groups)[:, None] * y, length)
    low = [jnp.asarray(v)[None, :, :] for v in low]
    high = [jnp.asarray(v)[:, None, :] for v in high]
    inner = [v.reshape(1, width, length) for v in turned(high, low)]
    outer = [jnp.take(jnp.asarray(v), order, axis=0)[:, None, :] for v in block]
    both = [v.reshape(groups * width, length).astype(jnp.bfloat16) for v in turned(outer, inner)]
    return lax.optimization_barrier(tuple(both))


def wave_operator(fields, kx, ky):
    (er, ei), (nr, ni), (hr, hi) = fields
    cx, cy = wave_speed * kx, wave_speed * ky
    return (
        (coriolis * nr + cx * hi, coriolis * ni - cx * hr),
        (cy * hi - coriolis * er, -coriolis * ei - cy * hr),
        (cx * ei + cy * ni, -(cx * er + cy * nr)),
    )


def wave_factors(kx, ky, phase):
    square = coriolis * coriolis + wave_speed * wave_speed * (kx * kx + ky * ky)
    frequency = jnp.sqrt(square)
    angle = frequency * phase
    return jnp.sin(angle) / frequency, (1.0 - jnp.cos(angle)) / square


def wave_exponential(fields, kx, ky, factors):
    sine, cosine = factors
    single = wave_operator(fields, kx, ky)
    double = wave_operator(single, kx, ky)
    return tuple(
        tuple(w + sine * a + cosine * b for w, a, b in zip(ws, one, two))
        for ws, one, two in zip(fields, single, double)
    )


def planes(fields):
    return tuple((fields[i, 0], fields[i, 1]) for i in range(fields.shape[0]))


def per_device(spectral_state, phase_index, weight_count):
    slots, owners = lax.axis_size("space"), lax.axis_size("avg")
    block, width = spectral_state.shape[2:]
    length, half = block * slots, block // 2
    chips = owners // 2
    g, a = lax.axis_index("space"), lax.axis_index("avg")
    low = g < slots // 2
    phase = phase_index[0].astype(jnp.float32) * phase_step
    weight = weight_count[0].astype(jnp.float32) / (weight_scale * owners)

    xor = jnp.array([2 * m + c for c in range(2) for m in range(chips)], jnp.int32)
    order = a ^ xor
    columns = (order[:, None] * width + jnp.arange(width, dtype=jnp.int32)).reshape(1, -1)
    ky = wave_of(columns, length)
    cosine_table, sine_table = column_tables(length, width, owners, order)
    packed = jnp.asarray(packed_table(length, slots))

    base = jnp.where(low, 2 * half * g, 2 * half * (slots - 1 - g) + half)
    direct = base + jnp.arange(half, dtype=jnp.int32)
    mirror = jnp.where(direct == 0, length // 2, length - direct)
    kx = wave_of(jnp.concatenate([direct, mirror])[:, None], length)
    self_paired = (direct == 0)[:, None]

    def flip(values, step):
        return lax.ppermute(values, "avg", [(i, i ^ step) for i in range(owners)])

    swap = [(i, slots - 1 - i) for i in range(slots)]
    edge = [(0, slots // 2)] + [(i, slots - i) for i in range(1, slots // 2)]

    r = np.arange(half)
    into = np.zeros((2, block, half + 8 + block), np.float32)
    into[0, r, half + 8 + r] = 1
    into[0, half + r[1:], half - r[1:]] = 1
    into[0, half, half] = 1
    into[1, r, r] = 1
    into[1, half + r, half + 8 + half - r] = 1
    into = jnp.where(low, into[0], into[1]).astype(jnp.bfloat16)
    narrow = spectral_state.astype(jnp.bfloat16)
    received = lax.ppermute(narrow[:, :, half:], "space", swap)
    corner = lax.ppermute(narrow[:, :, :8], "space", [(t, s) for s, t in edge])
    rows = jnp.concatenate([received, corner, narrow], axis=2)
    mine = jnp.einsum("rk,fckn->fcrn", into, rows, preferred_element_type=jnp.float32)
    mine = mine.astype(jnp.bfloat16)
    same = jnp.concatenate([mine] + [flip(mine, 2 * m) for m in range(1, chips)], axis=3)
    gathered = jnp.concatenate([same, flip(same, 1)], axis=3).astype(jnp.float32)

    forward_factors = lax.optimization_barrier(wave_factors(kx, ky, phase))
    rotated = wave_exponential(planes(gathered), kx, ky, forward_factors)
    cosine_rows, sine_rows = [], []
    parts = []
    for real, imag in rotated:
        re1, re2 = real[:half], real[half:]
        im1, im2 = imag[:half], imag[half:]
        parts.append((
            jnp.where(self_paired, re1, re1 + re2),
            jnp.where(self_paired, re2, im1 - im2),
            jnp.where(self_paired, -im1, -(im1 + im2)),
            jnp.where(self_paired, -im2, re1 - re2),
        ))
    cosine_rows = jnp.stack([jnp.stack([p[c] for p in parts]) for c in range(2)]).astype(jnp.bfloat16)
    sine_rows = jnp.stack([jnp.stack([p[2 + c] for p in parts]) for c in range(2)]).astype(jnp.bfloat16)
    half_done = (
        jnp.einsum("cfkn,ny->cfky", cosine_rows, cosine_table, preferred_element_type=jnp.float32)
        + jnp.einsum("cfkn,ny->cfky", sine_rows, sine_table, preferred_element_type=jnp.float32)
    ).astype(jnp.bfloat16)
    outgoing = half_done.reshape(2, 3, half, slots, block).transpose(3, 0, 1, 2, 4)
    arrived = lax.all_to_all(outgoing, "space", split_axis=0, concat_axis=0, tiled=True)
    physical = jnp.einsum(
        "pckx,pcfky->xfy", packed, arrived, preferred_element_type=jnp.float32
    ) * (1.0 / length)
    east, north, height = physical[:, 0], physical[:, 1], physical[:, 2]
    products = jnp.stack(
        [east * east, east * north, north * north, east * height, north * height], axis=1
    ).astype(jnp.bfloat16)
    forward_half = jnp.einsum(
        "gcrx,xqy->gcrqy", packed, products, preferred_element_type=jnp.float32
    ).astype(jnp.bfloat16)
    returned = lax.all_to_all(forward_half, "space", split_axis=0, concat_axis=0, tiled=True)
    returned = returned.transpose(3, 1, 2, 0, 4).reshape(5, 2, half, length)
    by_cosine = jnp.einsum(
        "qcry,ny->qcrn", returned, cosine_table, preferred_element_type=jnp.float32
    )
    by_sine = jnp.einsum(
        "qcry,ny->qcrn", returned, sine_table, preferred_element_type=jnp.float32
    )
    rc, ic = by_cosine[:, 0], by_cosine[:, 1]
    rs, isn = by_sine[:, 0], by_sine[:, 1]
    scale = weight / length
    real = scale * jnp.concatenate(
        [jnp.where(self_paired, rc, rc + isn), jnp.where(self_paired, ic, rc - isn)], axis=1
    )
    imag = scale * jnp.concatenate(
        [jnp.where(self_paired, -rs, ic - rs), jnp.where(self_paired, -isn, -ic - rs)], axis=1
    )
    tendency = tuple(
        (kx * imag[i] + ky * imag[j], -(kx * real[i] + ky * real[j]))
        for i, j in ((0, 1), (1, 2), (3, 4))
    )
    back = wave_exponential(tendency, kx, ky, (-forward_factors[0], forward_factors[1]))
    back = jnp.stack([jnp.stack(p) for p in back]).astype(jnp.bfloat16)

    split = chips * width
    near = back[..., :split].astype(jnp.float32) + flip(back[..., split:], 1).astype(jnp.float32)
    sent = near.astype(jnp.bfloat16)
    total = near[..., :width]
    for m in range(1, chips):
        total = total + flip(sent[..., m * width : (m + 1) * width], 2 * m).astype(jnp.float32)
    summed = total.astype(jnp.bfloat16)

    out = np.zeros((2, block, half + half + 8), np.float32)
    out[0, r, r] = 1
    out[0, half + r, half + r] = 1
    out[1, half - r, r] = 1
    out[1, block - r[1:], half + r[1:]] = 1
    out[1, 0, 2 * half] = 1
    out = jnp.where(low, out[0], out[1]).astype(jnp.bfloat16)
    first, second = summed[:, :, :half], summed[:, :, half:]
    own = jnp.where(low, first, second)
    other = lax.ppermute(jnp.where(low, second, first), "space", swap)
    corner = lax.ppermute(second[:, :, :8], "space", edge)
    rows = jnp.concatenate([own, other, corner], axis=2)
    averaged = jnp.einsum("rk,fckn->fcrn", out, rows, preferred_element_type=jnp.float32)

    own_rows = wave_of(g * block + jnp.arange(block, dtype=jnp.int32)[:, None], length)
    own_columns = ky[:, :width]
    state = spectral_state + time_step * averaged
    factors = wave_factors(own_rows, own_columns, time_step)
    advanced = wave_exponential(planes(state), own_rows, own_columns, factors)
    return jnp.stack([jnp.stack(p) for p in advanced])


def solution(mesh):
    in_specs = (P(None, None, "space", "avg"), P("avg"), P("avg"))
    out_specs = P(None, None, "space", "avg")
    return jax.shard_map(
        per_device, mesh=mesh, in_specs=in_specs, out_specs=out_specs, check_vma=False
    )
```

profile of v0, /device:TPU:26, one launch (start us, length us, event | category | flops | bytes accessed | tf_op | source)
XLA Modules:
  0.0 177.9 jit_solution(5790444581123222336)
XLA Ops:
  0.0 1.2 convert_element_type.113
  1.2 1.2 collective-permute-start
  2.4 3.6 %collective-permute-start.1 = (bf16[3,2,8,256]{3,2,1,0:T(8,128)(2,1)S(1)}, bf16[3,2,8,256]{3,2,1,0:T(8,128)(2,1)S(1)}, u32[]{:S(2)}, u32[]{:S(2)}) collective-permute-start(bf16[3,2,8,256]{3,2,1,0:T(8,128)(2,1)S(1)} %slice.212), channel_id=1, source_target_pairs={{4,0},{7,1},{6,2},{5,3},{12,8},{15,9},{14,10},{13,11},{20,16},{23,... | collective-permute-start | bytes 73736 | tf_op jit(solution)/shard_map/ppermute | solution.py:129
  6.0 0.7 xor_multiply_fusion
  6.7 0.7 compare_and_fusion
  7.4 0.1 fusion.92
  7.5 0.1 broadcast_multiply_fusion.5
  8.2 1.3 gather_fusion
  9.5 1.3 gather_fusion.1
  10.9 1.3 fusion.23
  12.2 0.6 collective-permute-start.2
  12.8 2.1 %subtract_divide_fusion = (f32[128,1024]{0,1:T(8,128)S(1)}, f32[128,1024]{0,1:T(8,128)S(1)}) fusion(f32[]{:T(128)} %bitcast.5, f32[1024]{0:T(1024)S(1)} %get-tuple-element.70, f32[128]{0:T(128)S(1)} %get-tuple-element.83), kind=kLoop, calls=%fused_computation.144 | loop fusion | flops 917504 | bytes 1053188 | tf_op jit(solution)/shard_map/div | solution.py:73
  15.0 7.6 %collective-permute-done.2 = bf16[3,2,128,256]{2,3,1,0:T(8,128)(2,1)S(1)} collective-permute-done((bf16[3,2,128,256]{2,3,1,0:T(8,128)(2,1)S(1)}, bf16[3,2,128,256]{2,3,1,0:T(8,128)(2,1)S(1)}, u32[]{:S(2)}, u32[]{:S(2)}) %collective-permute-start.2) | collective-permute-done | bytes 393248 | tf_op jit(solution)/shard_map/ppermute | solution.py:114
  22.6 0.1 collective-permute-start.3
  22.7 0.1 broadcast_select_fusion.3
  22.8 0.3 multiply_subtract_fusion
  23.1 1.2 add_convert_fusion
  24.3 0.7 collective-permute-done.3
  25.0 0.2 maximum_convert_fusion
  25.2 0.9 multiply_add_fusion.6
  26.1 0.3 multiply_add_fusion.10
  26.5 0.3 fusion.72
  26.8 0.6 fusion.73
  27.4 0.7 fusion.57
  28.1 0.2 maximum_bitcast_fusion
  28.3 0.2 maximum_bitcast_fusion.1
  28.5 0.2 maximum_bitcast_fusion.2
  28.7 0.2 maximum_bitcast_fusion.3
  28.9 1.0 fusion
  30.0 1.0 add_convert_fusion.1
  31.0 0.2 copy.75
  31.2 0.2 copy.78
  31.4 24.9 %all_to_all.10 = bf16[8,2,3,64,128]{4,3,1,2,0:T(8,128)(2,1)S(1)} all-to-all(bf16[8,2,3,64,128]{4,3,1,2,0:T(8,128)(2,1)S(1)} %bitcast.491), channel_id=1, replica_groups=mesh['avg'=4,'space'=8] {'space'}, dimensions={0} | all-to-all | bytes 1572864 | tf_op jit(solution)/shard_map/all_to_all | solution.py:156
  56.2 1.0 fusion.14
  57.5 1.3 copy-done.8
  58.9 1.8 %fusion.19 = bf16[8,2,64,5,128]{4,2,1,0,3:T(8,128)(2,1)S(1)} fusion(bf16[8,2,64,1024,1]{3,2,1,0,4:T(8,128)(2,1)S(1)} %copy-done.8, bf16[1024,5,128]{0,2,1:T(8,128)(2,1)S(1)} %fusion.70), kind=kOutput, calls=%fused_computation.35 | convolution fusion | flops 1342832640 | bytes 4718592 | tf_op jit(solution)/shard_map/gcrx,xqy->gcrqy/dot_general | solution.py:164
  60.7 1.2 copy.47
  61.9 6.6 %all-to-all-start.1 = ((bf16[8,2,64,5,128]{4,2,1,3,0:T(8,128)(2,1)}), bf16[8,2,64,5,128]{4,2,1,3,0:T(8,128)(2,1)}, u32[]{:S(2)}, u32[]{:S(2)}) async-start(bf16[8,2,64,5,128]{4,2,1,3,0:T(8,128)(2,1)} %copy.47), calls=%async_computation.1 | async-start | bytes 2621440 | tf_op jit(solution)/shard_map/all_to_all | solution.py:167
  69.2 27.5 %all-to-all-done.1 = bf16[8,2,64,5,128]{4,2,1,3,0:T(8,128)(2,1)} async-done(((bf16[8,2,64,5,128]{4,2,1,3,0:T(8,128)(2,1)}), bf16[8,2,64,5,128]{4,2,1,3,0:T(8,128)(2,1)}, u32[]{:S(2)}, u32[]{:S(2)}) %all-to-all-start.1) | async-done | bytes 1310752 | tf_op jit(solution)/shard_map/all_to_all | solution.py:167
  96.6 3.4 %copy.72 = bf16[5,2,64,8,128]{4,3,2,0,1:T(8,128)(2,1)} copy(bf16[5,2,64,8,128]{4,2,1,0,3:T(8,128)(2,1)} %bitcast.43) | data formatting | bytes 2621440 | tf_op jit(solution)/shard_map/reshape | solution.py:168
  100.0 3.3 %reshape.1676 = bf16[5,2,64,1024]{3,2,0,1:T(8,128)(2,1)} reshape(bf16[5,2,64,8,128]{4,3,2,0,1:T(8,128)(2,1)} %copy.72) | data formatting | bytes 2621440 | tf_op jit(solution)/shard_map/reshape | solution.py:168
  103.2 6.4 %fusion.4 = f32[5,2,64,1024]{2,3,0,1:T(8,128)} fusion(bf16[5,2,64,1024]{3,2,0,1:T(8,128)(2,1)} %reshape.1676, bf16[1024,1024]{1,0:T(8,128)(2,1)} %bitcast.487), kind=kOutput, calls=%fused_computation.18 | convolution fusion | flops 1342177280 | bytes 6029312 | tf_op jit(solution)/shard_map/qcry,ny->qcrn/dot_general | solution.py:172
  109.7 4.6 %fusion.6 = f32[5,2,64,1024]{2,3,0,1:T(8,128)} fusion(bf16[5,2,64,1024]{3,2,0,1:T(8,128)(2,1)S(1)} %copy-done.3, bf16[1024,1024]{1,0:T(8,128)(2,1)S(1)} %bitcast.485), kind=kOutput, calls=%fused_computation.20 | convolution fusion | flops 1342177280 | bytes 6029312 | tf_op jit(solution)/shard_map/qcry,ny->qcrn/dot_general | solution.py:169
  114.3 5.4 %add_select_fusion = (f32[5,64,1024]{1,2,0:T(8,128)S(1)}, f32[5,64,1024]{1,2,0:T(8,128)S(1)}, f32[5,64,1024]{1,2,0:T(8,128)S(1)}, f32[5,64,1024]{1,2,0:T(8,128)S(1)}) fusion(f32[5,2,64,1024]{2,3,0,1:T(8,128)} %fusion.6, f32[5,2,64,1024]{2,3,0,1:T(8,128)} %fusion.4, pred[64]{0:T(512)(128)(4,1)S(1)} %broadcast_compare_fusion), kind=kLoop, calls=%fused_computation.4 | loop fusion | flops 3604480 | bytes 10485824 | tf_op jit(solution)/shard_map/jit(_where)/select_n | solution.py:179
  119.7 0.7 maximum_multiply_fusion
  120.4 0.7 maximum_multiply_fusion.1
  121.2 1.3 fusion.75
  122.6 0.9 fusion.76
  123.6 0.2 pad_maximum_fusion
  123.9 2.3 %collective-permute-done.4 = bf16[3,2,128,512]{2,3,1,0:T(8,128)(2,1)S(1)} collective-permute-done((bf16[3,2,128,512]{2,3,1,0:T(8,128)(2,1)S(1)}, bf16[3,2,128,512]{2,3,1,0:T(8,128)(2,1)S(1)}, u32[]{:S(2)}, u32[]{:S(2)}) %collective-permute-start.4) | collective-permute-done | bytes 786464 | tf_op jit(solution)/shard_map/ppermute | solution.py:114
  126.2 0.2 convert_add_fusion
  126.4 0.6 collective-permute-start.5
  127.1 10.6 %collective-permute-done.5 = bf16[3,2,128,256]{2,3,1,0:T(8,128)(2,1)S(1)} collective-permute-done((bf16[3,2,128,256]{2,3,1,0:T(8,128)(2,1)S(1)}, bf16[3,2,128,256]{2,3,1,0:T(8,128)(2,1)S(1)}, u32[]{:S(2)}, u32[]{:S(2)}) %collective-permute-start.5) | collective-permute-done | bytes 393248 | tf_op jit(solution)/shard_map/ppermute | solution.py:114
  137.7 0.1 fusion.24
  137.8 0.2 broadcast_select_fusion.1
  137.9 3.6 %collective-permute-start.6 = (bf16[3,2,64,256]{2,3,1,0:T(8,128)(2,1)S(1)}, bf16[3,2,64,256]{2,3,1,0:T(8,128)(2,1)S(1)}, u32[]{:S(2)}, u32[]{:S(2)}) collective-permute-start(bf16[3,2,64,256]{2,3,1,0:T(8,128)(2,1)S(1)} %get-tuple-element.64), channel_id=1, source_target_pairs={{0,7},{1,6},{2,5},{3,4},{4,3},{5,2},{6,1},{7,0},{8,15},{9,14},{10,... | collective-permute-start | bytes 589832 | tf_op jit(solution)/shard_map/ppermute | solution.py:208
  141.5 0.2 slice.254
  141.7 1.5 collective-permute-start.7
  143.3 0.3 copy.54
  143.5 30.2 %collective-permute-done.7 = bf16[3,2,8,256]{2,3,1,0:T(8,128)(2,1)S(1)} collective-permute-done((bf16[3,2,8,256]{2,3,1,0:T(8,128)(2,1)S(1)}, bf16[3,2,8,256]{2,3,1,0:T(8,128)(2,1)S(1)}, u32[]{:S(2)}, u32[]{:S(2)}) %collective-permute-start.7) | collective-permute-done | bytes 24608 | tf_op jit(solution)/shard_map/ppermute | solution.py:209
  173.7 1.3 fusion.22
  175.0 0.8 multiply_add_fusion.19
  175.9 0.7 multiply_add_fusion.15
  176.7 1.1 copy.55
  (49 shorter events, 0.9 us)
Async XLA Ops:
  1.2 9.7 %collective-permute-start = (bf16[3,2,64,256]{3,2,1,0:T(8,128)(2,1)S(1)}, bf16[3,2,64,256]{3,2,1,0:T(8,128)(2,1)S(1)}, u32[]{:S(2)}, u32[]{:S(2)}) collective-permute-start(bf16[3,2,64,256]{3,2,1,0:T(8,128)(2,1)S(1)} %slice.211), channel_id=1, source_target_pairs={{0,7},{1,6},{2,5},{3,4},{4,3},{5,2},{6,1},{7,0},{8,15},{9,14},{10,... | collective-permute-start | bytes 589832 | tf_op jit(solution)/shard_map/ppermute | solution.py:128
  2.4 8.5 %collective-permute-start.1 = (bf16[3,2,8,256]{3,2,1,0:T(8,128)(2,1)S(1)}, bf16[3,2,8,256]{3,2,1,0:T(8,128)(2,1)S(1)}, u32[]{:S(2)}, u32[]{:S(2)}) collective-permute-start(bf16[3,2,8,256]{3,2,1,0:T(8,128)(2,1)S(1)} %slice.212), channel_id=1, source_target_pairs={{4,0},{7,1},{6,2},{5,3},{12,8},{15,9},{14,10},{13,11},{20,16},{23,... | collective-permute-start | bytes 73736 | tf_op jit(solution)/shard_map/ppermute | solution.py:129
  10.8 11.9 %copy-start.4 = (f32[16,1024]{1,0:T(8,128)S(1)}, f32[16,1024]{1,0:T(8,128)}, u32[]{:S(2)}) copy-start(f32[16,1024]{1,0:T(8,128)} %constant.126.clone) | copy-start | bytes 196612
  10.9 11.9 %copy-start.5 = (f32[16,1024]{1,0:T(8,128)S(1)}, f32[16,1024]{1,0:T(8,128)}, u32[]{:S(2)}) copy-start(f32[16,1024]{1,0:T(8,128)} %constant.127.clone) | copy-start | bytes 196612
  10.9 11.9 %copy-start.6 = (f32[16,1024]{1,0:T(8,128)S(1)}, f32[16,1024]{1,0:T(8,128)}, u32[]{:S(2)}) copy-start(f32[16,1024]{1,0:T(8,128)} %constant.128.clone) | copy-start | bytes 196612
  10.9 11.9 %copy-start.7 = (f32[16,1024]{1,0:T(8,128)S(1)}, f32[16,1024]{1,0:T(8,128)}, u32[]{:S(2)}) copy-start(f32[16,1024]{1,0:T(8,128)} %constant.129.clone) | copy-start | bytes 196612
  12.2 10.4 %collective-permute-start.2 = (bf16[3,2,128,256]{2,3,1,0:T(8,128)(2,1)S(1)}, bf16[3,2,128,256]{2,3,1,0:T(8,128)(2,1)S(1)}, u32[]{:S(2)}, u32[]{:S(2)}) collective-permute-start(bf16[3,2,128,256]{2,3,1,0:T(8,128)(2,1)S(1)} %fusion.23), channel_id=1, source_target_pairs={{0,16},{8,24},{16,0},{24,8},{1,17},{9,25},{17,1},{25,9},{2,18},{10... | collective-permute-start | bytes 1179656 | tf_op jit(solution)/shard_map/ppermute | solution.py:114
  22.6 2.4 %collective-permute-start.3 = (bf16[3,2,128,512]{2,3,1,0:T(8,128)(2,1)S(1)}, bf16[3,2,128,512]{2,3,1,0:T(8,128)(2,1)S(1)}, u32[]{:S(2)}, u32[]{:S(2)}) collective-permute-start(bf16[3,2,128,512]{2,3,1,0:T(8,128)(2,1)S(1)} %pad_maximum_fusion.1), channel_id=1, source_target_pairs={{0,8},{8,0},{16,24},{24,16},{1,9},{9,1},{17,25},{25,17},{2,10},{10... | collective-permute-start | bytes 2359304 | tf_op jit(solution)/shard_map/ppermute | solution.py:114
  24.3 4.7 %copy-start = (bf16[4,256,1024]{2,1,0:T(8,128)(2,1)}, bf16[4,256,1024]{2,1,0:T(8,128)(2,1)S(1)}, u32[]{:S(2)}) copy-start(bf16[4,256,1024]{2,1,0:T(8,128)(2,1)S(1)} %get-tuple-element.45) | copy-start | bytes 6291460
  31.0 25.2 %copy-start.2 = (bf16[8,2,64,1024,1]{3,2,1,4,0:T(8,128)(2,1)S(1)}, bf16[8,2,64,1024,1]{3,2,1,4,0:T(8,128)(2,1)}, u32[]{:S(2)}) copy-start(bf16[8,2,64,1024,1]{3,2,1,4,0:T(8,128)(2,1)} %constant.140) | copy-start | bytes 6291460
  57.3 1.6 copy-start.8
  61.9 34.7 %all-to-all-start.1 = ((bf16[8,2,64,5,128]{4,2,1,3,0:T(8,128)(2,1)}), bf16[8,2,64,5,128]{4,2,1,3,0:T(8,128)(2,1)}, u32[]{:S(2)}, u32[]{:S(2)}) async-start(bf16[8,2,64,5,128]{4,2,1,3,0:T(8,128)(2,1)} %copy.47), calls=%async_computation.1 | async-start | bytes 2621440 | tf_op jit(solution)/shard_map/all_to_all | solution.py:167
  103.2 6.4 %copy-start.3 = (bf16[5,2,64,1024]{3,2,0,1:T(8,128)(2,1)S(1)}, bf16[5,2,64,1024]{3,2,0,1:T(8,128)(2,1)}, u32[]{:S(2)}) copy-start(bf16[5,2,64,1024]{3,2,0,1:T(8,128)(2,1)} %reshape.1676) | copy-start | bytes 3932164
  123.8 2.4 %collective-permute-start.4 = (bf16[3,2,128,512]{2,3,1,0:T(8,128)(2,1)S(1)}, bf16[3,2,128,512]{2,3,1,0:T(8,128)(2,1)S(1)}, u32[]{:S(2)}, u32[]{:S(2)}) collective-permute-start(bf16[3,2,128,512]{2,3,1,0:T(8,128)(2,1)S(1)} %slice.249), channel_id=1, source_target_pairs={{0,8},{8,0},{16,24},{24,16},{1,9},{9,1},{17,25},{25,17},{2,10},{10... | collective-permute-start | bytes 2359304 | tf_op jit(solution)/shard_map/ppermute | solution.py:114
  126.4 16.8 %copy-start.1 = (f32[3,2,128,256]{3,2,1,0:T(8,128)S(1)}, f32[3,2,128,256]{3,2,1,0:T(8,128)}, u32[]{:S(2)}) copy-start(f32[3,2,128,256]{3,2,1,0:T(8,128)} %param.17) | copy-start | bytes 2359300
  126.4 11.2 %collective-permute-start.5 = (bf16[3,2,128,256]{2,3,1,0:T(8,128)(2,1)S(1)}, bf16[3,2,128,256]{2,3,1,0:T(8,128)(2,1)S(1)}, u32[]{:S(2)}, u32[]{:S(2)}) collective-permute-start(bf16[3,2,128,256]{2,3,1,0:T(8,128)(2,1)S(1)} %slice.694), channel_id=1, source_target_pairs={{0,16},{8,24},{16,0},{24,8},{1,17},{9,25},{17,1},{25,9},{2,18},{10... | collective-permute-start | bytes 1179656 | tf_op jit(solution)/shard_map/ppermute | solution.py:114
  137.9 35.8 %collective-permute-start.6 = (bf16[3,2,64,256]{2,3,1,0:T(8,128)(2,1)S(1)}, bf16[3,2,64,256]{2,3,1,0:T(8,128)(2,1)S(1)}, u32[]{:S(2)}, u32[]{:S(2)}) collective-permute-start(bf16[3,2,64,256]{2,3,1,0:T(8,128)(2,1)S(1)} %get-tuple-element.64), channel_id=1, source_target_pairs={{0,7},{1,6},{2,5},{3,4},{4,3},{5,2},{6,1},{7,0},{8,15},{9,14},{10,... | collective-permute-start | bytes 589832 | tf_op jit(solution)/shard_map/ppermute | solution.py:208
  141.7 32.0 %collective-permute-start.7 = (bf16[3,2,8,256]{2,3,1,0:T(8,128)(2,1)S(1)}, bf16[3,2,8,256]{2,3,1,0:T(8,128)(2,1)S(1)}, u32[]{:S(2)}, u32[]{:S(2)}) collective-permute-start(bf16[3,2,8,256]{2,3,1,0:T(8,128)(2,1)S(1)} %slice.254), channel_id=1, source_target_pairs={{0,4},{1,7},{2,6},{3,5},{8,12},{9,15},{10,14},{11,13},{16,20},{17,... | collective-permute-start | bytes 73736 | tf_op jit(solution)/shard_map/ppermute | solution.py:209
where the time goes:
time: 179 us; the launch traced here: 178 us
  waiting for transfers between devices  78.8 us (44%)
  blocking collectives  24.9 us (14%)
  other arithmetic  22.1 us (12%)
  matrix products  18.5 us (10%)
  starting transfers between devices  17.9 us (10%)
  local copies, waits for them, and re-layouts  13.9 us (8%)
  between operations  1.88 us (1%)
    ppermute x1, waiting for transfers between devices, per_device(): corner = lax.ppermute(second[:, :, :8], 'space', edge)  30.2 us
    all_to_all x1, waiting for transfers between devices, per_device(): lax.all_to_all(forward_half, 'space', split_axis=0, concat_axis=0, tiled=...  27.5 us
    all_to_all x1, blocking collectives, per_device(): lax.all_to_all(outgoing, 'space', split_axis=0, concat_axis=0, tiled=True)  24.9 us
    ppermute x4, waiting for transfers between devices, flip(): return lax.ppermute(values, 'avg', [(i, i ^ step) for i in range(owners)])  21.1 us
    all_to_all x1, starting transfers between devices, per_device(): lax.all_to_all(forward_half, 'space', split_axis=0, concat_axis=0, tiled=...  6.62 us
    reshape x2, local copies, waits for them, and re-layouts, per_device(): returned = returned.transpose(3, 1, 2, 0, 4).reshape(5, 2, half, length)  6.61 us
    dot_general x1, matrix products, per_device(): jnp.einsum('qcry,ny->qcrn', returned, sine_table, preferred_element_type=...  6.4 us
    select_n x1, other arithmetic, per_device(): jnp.where(self_paired, rc, rc + isn)  5.4 us
  transfers between devices with their start and end apart: 9, of which 6 were waited for; matrix products, arithmetic and copies ran while one was open for 5% of the time, Pallas kernels for 0%

commit v1 on v0

v1 whole, which is shorter than its diff:
```python
import functools

import jax
import jax.numpy as jnp
import ml_dtypes
import numpy as np
from jax import lax
from jax.experimental import pallas as pl
from jax.experimental.pallas import tpu as pltpu
from jax.sharding import PartitionSpec as P

coriolis = 1.0
wave_speed = 6.0
phase_step = 0.25
time_step = 2.0
weight_scale = 4.0


def wave_of(positions, length):
    shifted = (positions + length // 2) % length - length // 2
    return shifted.astype(jnp.float32) * (2.0 / length)


def circle(products, length):
    angles = (products % length) * (2.0 * np.pi / length)
    return np.cos(angles).astype(np.float32), np.sin(angles).astype(np.float32)


def slot_base(slot, slots, half):
    return np.where(slot < slots // 2, 2 * half * slot, 2 * half * (slots - 1 - slot) + half)


def packed_table(length, slots, chunks):
    half = length // (2 * slots)
    rows = slot_base(np.arange(slots), slots, half)[:, None] + np.arange(half)
    cosine, sine = circle(rows[:, :, None] * np.arange(length), length)
    packed = np.stack([cosine, -sine], axis=1)
    packed[0, 1, 0] = circle(length // 2 * np.arange(length), length)[0]
    packed = packed.reshape(slots, 2, chunks, half // chunks, length).transpose(2, 0, 1, 3, 4)
    return packed.reshape(length, length).astype(ml_dtypes.bfloat16)


def turned(first, second):
    (c, s), (d, t) = first, second
    return c * d - s * t, s * d + c * t


def column_tables(length, width, groups, order):
    fine = 1
    while fine * fine < width:
        fine *= 2
    y = np.arange(length)
    low = circle(np.arange(fine)[:, None] * y, length)
    high = circle(fine * np.arange(width // fine)[:, None] * y, length)
    block = circle(width * np.arange(groups)[:, None] * y, length)
    low = [jnp.asarray(v)[None, :, :] for v in low]
    high = [jnp.asarray(v)[:, None, :] for v in high]
    inner = [v.reshape(1, width, length) for v in turned(high, low)]
    outer = [jnp.take(jnp.asarray(v), order, axis=0)[:, None, :] for v in block]
    both = [v.reshape(groups * width, length).astype(jnp.bfloat16) for v in turned(outer, inner)]
    return lax.optimization_barrier(tuple(both))


def wave_operator(fields, kx, ky):
    (er, ei), (nr, ni), (hr, hi) = fields
    cx, cy = wave_speed * kx, wave_speed * ky
    return (
        (coriolis * nr + cx * hi, coriolis * ni - cx * hr),
        (cy * hi - coriolis * er, -coriolis * ei - cy * hr),
        (cx * ei + cy * ni, -(cx * er + cy * nr)),
    )


def wave_factors(kx, ky, phase):
    square = coriolis * coriolis + wave_speed * wave_speed * (kx * kx + ky * ky)
    frequency = jnp.sqrt(square)
    angle = frequency * phase
    return jnp.sin(angle) / frequency, (1.0 - jnp.cos(angle)) / square


def wave_exponential(fields, kx, ky, factors):
    sine, cosine = factors
    single = wave_operator(fields, kx, ky)
    double = wave_operator(single, kx, ky)
    return tuple(
        tuple(w + sine * a + cosine * b for w, a, b in zip(ws, one, two))
        for ws, one, two in zip(fields, single, double)
    )


def planes(fields):
    return tuple((fields[i, 0], fields[i, 1]) for i in range(fields.shape[0]))


MESH = pl.DeviceIdType.MESH
EDGE = 16


def column(info, t, index):
    return info[t, :, index : index + 1]


def positions():
    g, a = lax.axis_index("space"), lax.axis_index("avg")
    return g, a, a // 2, a % 2


def edge_partner(g, slots):
    aligned = 1 - (g % (slots // 2) + slots // 2 - 1) // (slots // 2)
    return ((slots - g) % slots + aligned * (slots // 2)) % slots


def greet(slots, chips, edges):
    g, a, q, core = positions()
    barrier = pltpu.get_barrier_semaphore()
    peers = [((g + d) % slots, a) for d in range(1, slots)]
    peers += [(g, 2 * q + 1 - core)]
    peers += [(g, 2 * ((q + m) % chips) + core) for m in range(1, chips)]
    if edges:
        across = edge_partner(g, slots)
        peers += [
            (across, 2 * ((q + m) % chips) + (core + c) % 2)
            for c in range(2) for m in range(chips) if c or m
        ]
    for space, avg in peers:
        pl.semaphore_signal(
            barrier, inc=1, device_id={"space": space, "avg": avg}, device_id_type=MESH
        )
    pl.semaphore_wait(barrier, len(peers))


def remote(src, dst, send, recv, space, avg):
    return pltpu.make_async_remote_copy(
        src_ref=src, dst_ref=dst, send_sem=send, recv_sem=recv,
        device_id={"space": space, "avg": avg}, device_id_type=MESH,
    )


def forward_kernel(
    dims, keep, send, edge, sine, cosine, info, ky, ct, st, out,
    gx, eg, rows_c, rows_s, stage,
    ex_s, ex_r, eg_s, eg_r, x_s, x_r, c_s, c_r, a_s, a_r, l_s,
):
    slots, chips, chunks, hb, width, block = dims
    length = slots * block
    g, a, q, core = positions()
    low, high = g < slots // 2, g >= slots // 2
    partner = 2 * q + 1 - core
    across = edge_partner(g, slots)
    greet(slots, chips, True)

    exchange = [
        remote(send.at[t], gx.at[t, 1, 0, 0], ex_s.at[t], ex_r.at[t], slots - 1 - g, a)
        for t in range(chunks)
    ]
    edges = [
        remote(edge, eg.at[c, m], eg_s.at[c, m], eg_r.at[c, m],
               across, 2 * ((q + chips - m) % chips) + (core + c) % 2)
        for c in range(2) for m in range(chips)
    ]

    def mine(t, s):
        return gx.at[t, 1, 0, 0] if s else keep.at[t]

    def over_chips(t, s, m):
        return remote(mine(t, s), gx.at[t, s, 0, m], x_s.at[t, s, m], x_r.at[t, s, m],
                      g, 2 * ((q + chips - m) % chips) + core)

    def over_cores(t, s, m):
        source = gx.at[t, s, 0, m] if m else mine(t, s)
        return remote(source, gx.at[t, s, 1, m], c_s.at[t, s, m], c_r.at[t, s, m], g, partner)

    def all_to_all(t, d):
        to = (g + d) % slots
        return remote(stage.at[t, to], out.at[t, g], a_s.at[t, d], a_r.at[t, d], to, a)

    exchange[0].start()

    @pl.when(high)
    def _():
        for copy in edges:
            copy.start()
        eg[...] = jnp.zeros_like(eg)

    for t in range(1, chunks):
        exchange[t].start()
    for t in range(chunks):
        for m in range(1, chips):
            over_chips(t, 0, m).start()
        over_cores(t, 0, 0).start()
    for t in range(chunks):
        for m in range(1, chips):
            over_chips(t, 0, m).wait_recv()
            over_cores(t, 0, m).start()
    for t in range(chunks):
        exchange[t].wait_recv()
        for m in range(1, chips):
            over_chips(t, 1, m).start()
        over_cores(t, 1, 0).start()
        for m in range(1, chips):
            over_chips(t, 1, m).wait_recv()
            over_cores(t, 1, m).start()
        if t == 0:
            @pl.when(low)
            def _():
                for copy in edges:
                    copy.wait_recv()
        for s in range(2):
            for m in range(chips):
                over_cores(t, s, m).wait_recv()
        own_pair = column(info, t, 2) > 0.5
        sign = column(info, t, 3)
        for j in range(2 * chips):
            c, m = divmod(j, chips)
            span = slice(j * width, (j + 1) * width)
            turned_rows = []
            for s in range(2):
                source = keep.at[t] if s + j == 0 else gx.at[t, s, c, m]
                fields = [[source[f, i].astype(jnp.float32) for i in range(2)] for f in range(3)]
                if s == 1 and t == 0:
                    put = column(info, t, 4)[:EDGE] > 0.5
                    for f in range(3):
                        for i in range(2):
                            top = jnp.where(put, eg[c, m, f, i].astype(jnp.float32), fields[f][i][:EDGE])
                            fields[f][i] = (
                                jnp.concatenate([top, fields[f][i][EDGE:]], axis=0) if hb > EDGE else top
                            )
                turned_rows.append(wave_exponential(
                    fields, column(info, t, s), ky[:, span], (sine[t, s, :, span], cosine[t, s, :, span])
                ))
            for f in range(3):
                (re0, im0), (re1, im1) = turned_rows[0][f], turned_rows[1][f]
                for i, value in enumerate((
                    jnp.where(own_pair, re0, re0 + re1), jnp.where(own_pair, re1, sign * (im0 - im1))
                )):
                    rows_c[(i * 3 + f) * hb : (i * 3 + f + 1) * hb, span] = value.astype(jnp.bfloat16)
                for i, value in enumerate((
                    jnp.where(own_pair, -im0, -(im0 + im1)), jnp.where(own_pair, -im1, sign * (re0 - re1))
                )):
                    rows_s[(i * 3 + f) * hb : (i * 3 + f + 1) * hb, span] = value.astype(jnp.bfloat16)
        tile = min(length, max(block, 256))
        for y in range(0, length, tile):
            value = (
                jnp.dot(rows_c[...], ct[:, y : y + tile], preferred_element_type=jnp.float32)
                + jnp.dot(rows_s[...], st[:, y : y + tile], preferred_element_type=jnp.float32)
            ).astype(jnp.bfloat16)
            for b in range(tile // block):
                for i in range(2):
                    for f in range(3):
                        stage[t, y // block + b, i * hb : (i + 1) * hb, f * block : (f + 1) * block] = (
                            value[(i * 3 + f) * hb : (i * 3 + f + 1) * hb, b * block : (b + 1) * block]
                        )
        for d in range(1, slots):
            all_to_all(t, d).start()
        pltpu.make_async_copy(stage.at[t, g], out.at[t, g], l_s.at[t]).start()
    for t in range(chunks):
        for d in range(1, slots):
            all_to_all(t, d).wait_recv()
        pltpu.make_async_copy(stage.at[t, g], out.at[t, g], l_s.at[t]).wait()
    for t in range(chunks):
        exchange[t].wait_send()
        for s in range(2):
            for m in range(1, chips):
                over_chips(t, s, m).wait_send()
            for m in range(chips):
                over_cores(t, s, m).wait_send()
        for d in range(1, slots):
            all_to_all(t, d).wait_send()

    @pl.when(high)
    def _():
        for copy in edges:
            copy.wait_send()


def backward_kernel(
    dims, fh, sine, cosine, info, ky, ct, st, own, other, edge,
    ret, lhs, stage, rsin, acc, xs, rx, fin,
    a_s, a_r, l_s, c_s, c_r, x_s, x_r, ex_s, ex_r, eg_s, eg_r,
):
    slots, chips, chunks, hb, width, block = dims
    g, a, q, core = positions()
    low, high = g < slots // 2, g >= slots // 2
    partner = 2 * q + 1 - core
    greet(slots, chips, False)

    def all_to_all(t, d):
        to = (g + d) % slots
        return remote(fh.at[t, to], ret.at[t, g], a_s.at[t, d], a_r.at[t, d], to, a)

    def over_cores(t):
        return remote(stage.at[t, 1], rsin.at[t], c_s.at[t], c_r.at[t], g, partner)

    def over_chips(t, m):
        return remote(xs.at[t, m], rx.at[t, m], x_s.at[t, m], x_r.at[t, m],
                      g, 2 * ((q + m) % chips) + core)

    def exchange(t):
        return remote(fin.at[t], other.at[t], ex_s.at[t], ex_r.at[t], slots - 1 - g, a)

    edges = remote(fin.at[0, :, :, :EDGE], edge, eg_s, eg_r, edge_partner(g, slots), a)

    for t in range(chunks):
        for d in range(1, slots):
            all_to_all(t, d).start()
        pltpu.make_async_copy(fh.at[t, g], ret.at[t, g], l_s.at[t]).start()

    @pl.when(low)
    def _():
        edge[...] = jnp.zeros_like(edge)

    for t in range(chunks):
        for d in range(1, slots):
            all_to_all(t, d).wait_recv()
        pltpu.make_async_copy(fh.at[t, g], ret.at[t, g], l_s.at[t]).wait()
        for p in range(slots):
            for k in range(5):
                lhs[k * 2 * hb : (k + 1) * 2 * hb, p * block : (p + 1) * block] = (
                    ret[t, p, :, k * block : (k + 1) * block]
                )
        own_pair = column(info, t, 2) > 0.5
        sign, scale = column(info, t, 3), column(info, t, 5)
        for j in range(2 * chips):
            c, m = divmod(j, chips)
            span = slice(j * width, (j + 1) * width)
            dims_nt = (((1,), (1,)), ((), ()))
            by_c = lax.dot_general(lhs[...], ct[span, :], dims_nt, preferred_element_type=jnp.float32)
            by_s = lax.dot_general(lhs[...], st[span, :], dims_nt, preferred_element_type=jnp.float32)

            def part(values, k, i):
                return values[(2 * k + i) * hb : (2 * k + i + 1) * hb]

            for s in range(2):
                turn = scale * sign if s == 0 else -scale * sign
                real, imag = [], []
                for k in range(5):
                    rc, ic = part(by_c, k, 0), part(by_c, k, 1)
                    rs, iz = part(by_s, k, 0), part(by_s, k, 1)
                    real.append(jnp.where(own_pair, scale * (ic if s else rc), scale * rc + turn * iz))
                    imag.append(jnp.where(own_pair, -scale * (iz if s else rs), turn * ic - scale * rs))
                kx, kyj = column(info, t, s), ky[:, span]
                tendency = [
                    (kx * imag[u] + kyj * imag[v], -(kx * real[u] + kyj * real[v]))
                    for u, v in ((0, 1), (1, 2), (3, 4))
                ]
                back = wave_exponential(
                    tendency, kx, kyj, (-sine[t, s, :, span], cosine[t, s, :, span])
                )
                for f in range(3):
                    for i in range(2):
                        stage[t, c, m, s, f, i] = back[f][i].astype(jnp.bfloat16)
        over_cores(t).start()
        over_cores(t).wait_recv()
        for m in range(1, chips):
            xs[t, m] = (
                stage[t, 0, m].astype(jnp.float32) + rsin[t, m].astype(jnp.float32)
            ).astype(jnp.bfloat16)
            over_chips(t, m).start()
        acc[...] = stage[t, 0, 0].astype(jnp.float32) + rsin[t, 0].astype(jnp.float32)
        for m in range(1, chips):
            over_chips(t, m).wait_recv()
            acc[...] += rx[t, m].astype(jnp.float32)
        fin[t] = acc[1].astype(jnp.bfloat16)
        exchange(t).start()
        if t == 0:
            @pl.when(low)
            def _():
                edges.start()
        own[t] = acc[0].astype(jnp.bfloat16)
    for t in range(chunks):
        exchange(t).wait_recv()

    @pl.when(high)
    def _():
        edges.wait_recv()

    for t in range(chunks):
        for d in range(1, slots):
            all_to_all(t, d).wait_send()
        over_cores(t).wait_send()
        for m in range(1, chips):
            over_chips(t, m).wait_send()
        exchange(t).wait_send()

    @pl.when(low)
    def _():
        edges.wait_send()


VMEM = pl.BlockSpec(memory_space=pltpu.VMEM)


def per_device(spectral_state, phase_index, weight_count):
    slots, owners = lax.axis_size("space"), lax.axis_size("avg")
    block, width = spectral_state.shape[2:]
    length, half = block * slots, block // 2
    chips = owners // 2
    chunks = max(1, half // CHUNK_ROWS)
    hb = half // chunks
    dims = (slots, chips, chunks, hb, width, block)
    g, a = lax.axis_index("space"), lax.axis_index("avg")
    q, core = a // 2, a % 2
    low = g < slots // 2
    phase = phase_index[0].astype(jnp.float32) * phase_step
    weight = weight_count[0].astype(jnp.float32) / (weight_scale * owners)

    m, c = jnp.arange(chips, dtype=jnp.int32), jnp.arange(2, dtype=jnp.int32)[:, None]
    order = (2 * ((q + m) % chips) + (core + c) % 2).reshape(-1)
    columns = (order[:, None] * width + jnp.arange(width, dtype=jnp.int32)).reshape(1, -1)
    ky = wave_of(columns, length)
    cosine_table, sine_table = column_tables(length, width, owners, order)
    packed = jnp.asarray(packed_table(length, slots, chunks))

    base = jnp.where(low, 2 * half * g, 2 * half * (slots - 1 - g) + half)
    direct = base + jnp.arange(half, dtype=jnp.int32)
    mirror = jnp.where(direct == 0, length // 2, length - direct)
    first = wave_of(jnp.where(low, direct, mirror), length)
    second = wave_of(jnp.where(low, mirror, direct), length)
    ones = jnp.ones((half,), jnp.float32)
    start = (jnp.arange(half) == 0) & low
    info = jnp.stack([
        first, second, (direct == 0).astype(jnp.float32), jnp.where(low, ones, -ones),
        start.astype(jnp.float32), ones * (weight / length), ones, ones,
    ], axis=1).reshape(chunks, hb, 8)
    rows = jnp.stack([first, second]).reshape(2, chunks, hb).transpose(1, 0, 2)[..., None]
    sine, cosine = lax.optimization_barrier(wave_factors(rows, ky, phase))

    r = np.arange(half)
    into = np.zeros((2, 2, half, block), np.float32)
    into[0, 0, r, r] = 1
    into[0, 1, r, half + r] = 1
    into[1, 0, r, half - r] = 1
    into[1, 1, r[1:], block - r[1:]] = 1
    into = jnp.where(low, into[0], into[1]).astype(jnp.bfloat16).reshape(2, chunks, hb, block)
    narrow = spectral_state.astype(jnp.bfloat16)
    pick = lambda which: jnp.einsum(
        "thk,fckn->tfchn", into[which], narrow, preferred_element_type=jnp.float32
    ).astype(jnp.bfloat16)
    keep, send = pick(0), pick(1)

    piece = (3, 2, hb, width)
    dma = pltpu.SemaphoreType.DMA
    vmem = lambda shape: pltpu.VMEM(shape, jnp.bfloat16)
    arrived = pl.pallas_call(
        functools.partial(forward_kernel, dims),
        out_shape=jax.ShapeDtypeStruct((chunks, slots, 2 * hb, 3 * block), jnp.bfloat16),
        in_specs=[VMEM] * 9,
        out_specs=VMEM,
        scratch_shapes=[
            vmem((chunks, 2, 2, chips) + piece),
            vmem((2, chips, 3, 2, EDGE, width)),
            vmem((6 * hb, length)),
            vmem((6 * hb, length)),
            vmem((chunks, slots, 2 * hb, 3 * block)),
            dma((chunks,)), dma((chunks,)),
            dma((2, chips)), dma((2, chips)),
            dma((chunks, 2, chips)), dma((chunks, 2, chips)),
            dma((chunks, 2, chips)), dma((chunks, 2, chips)),
            dma((chunks, slots)), dma((chunks, slots)),
            dma((chunks,)),
        ],
        compiler_params=pltpu.CompilerParams(
            collective_id=0, has_side_effects=True, vmem_limit_bytes=48 * 2**20
        ),
        name="spectral_to_grid",
    )(keep, send, narrow[:, :, :EDGE], sine, cosine, info, ky, cosine_table, sine_table)

    physical = lax.dot_general(
        packed, arrived.reshape(length, 3 * block), (((0,), (0,)), ((), ())),
        preferred_element_type=jnp.float32,
    ) * (1.0 / length)
    east, north, height = (physical[:, i * block : (i + 1) * block] for i in range(3))
    products = jnp.concatenate(
        [east * east, east * north, north * north, east * height, north * height], axis=1
    ).astype(jnp.bfloat16)
    forward_half = jnp.dot(packed, products, preferred_element_type=jnp.float32).astype(jnp.bfloat16)
    forward_half = forward_half.reshape(chunks, slots, 2 * hb, 5 * block)

    own, other, edge = pl.pallas_call(
        functools.partial(backward_kernel, dims),
        out_shape=[
            jax.ShapeDtypeStruct((chunks,) + piece, jnp.bfloat16),
            jax.ShapeDtypeStruct((chunks,) + piece, jnp.bfloat16),
            jax.ShapeDtypeStruct((3, 2, EDGE, width), jnp.bfloat16),
        ],
        in_specs=[VMEM] * 7,
        out_specs=[VMEM] * 3,
        scratch_shapes=[
            vmem((chunks, slots, 2 * hb, 5 * block)),
            vmem((10 * hb, length)),
            vmem((chunks, 2, chips, 2) + piece),
            vmem((chunks, chips, 2) + piece),
            pltpu.VMEM((2,) + piece, jnp.float32),
            vmem((chunks, chips, 2) + piece),
            vmem((chunks, chips, 2) + piece),
            vmem((chunks,) + piece),
            dma((chunks, slots)), dma((chunks, slots)), dma((chunks,)),
            dma((chunks,)), dma((chunks,)),
            dma((chunks, chips)), dma((chunks, chips)),
            dma((chunks,)), dma((chunks,)),
            dma(()), dma(()),
        ],
        compiler_params=pltpu.CompilerParams(
            collective_id=1, has_side_effects=True, vmem_limit_bytes=48 * 2**20
        ),
        name="grid_to_spectral",
    )(forward_half, sine, cosine, info, ky, cosine_table, sine_table)

    back = np.zeros((2, block, 2 * half + EDGE), np.float32)
    back[0, r, r] = 1
    back[0, half + r, half + r] = 1
    back[1, half - r, r] = 1
    back[1, block - r[1:], half + r[1:]] = 1
    back[1, 0, 2 * half] = 1
    back = jnp.where(low, back[0], back[1]).astype(jnp.bfloat16)
    tall = lambda v: v.transpose(1, 2, 0, 3, 4).reshape(3, 2, half, width)
    stacked = jnp.concatenate([tall(own), tall(other), edge], axis=2)
    averaged = jnp.einsum("rk,fckn->fcrn", back, stacked, preferred_element_type=jnp.float32)

    own_rows = wave_of(g * block + jnp.arange(block, dtype=jnp.int32)[:, None], length)
    own_columns = ky[:, :width]
    state = spectral_state + time_step * averaged
    factors = wave_factors(own_rows, own_columns, time_step)
    advanced = wave_exponential(planes(state), own_rows, own_columns, factors)
    return jnp.stack([jnp.stack(p) for p in advanced])


CHUNK_ROWS = 32


def solution(mesh):
    in_specs = (P(None, None, "space", "avg"), P("avg"), P("avg"))
    out_specs = P(None, None, "space", "avg")
    return jax.shard_map(
        per_device, mesh=mesh, in_specs=in_specs, out_specs=out_specs, check_vma=False
    )
```

time: 179 us -> 129 us (0.72)
  the two profiles are of different devices: /device:TPU:26 before, /device:TPU:0 now
where the time goes in v1:
time: 129 us
  Pallas kernels  104 us (81%)
  other arithmetic  9.3 us (7%)
  local copies, waits for them, and re-layouts  9.21 us (7%)
  matrix products  4.46 us (3%)
  between operations  1.76 us (1%)
    pallas_call x1, Pallas kernels, per_device(): pl.pallas_call(functools.partial(backward_kernel, dims), out_shape=[jax.S...  59 us
    pallas_call x1, Pallas kernels, per_device(): pl.pallas_call(functools.partial(forward_kernel, dims), out_shape=jax.Sha...  45.2 us
    unnamed x21, local copies, waits for them, and re-layouts  3.52 us
    dot_general x1, matrix products, per_device(): jnp.dot(packed, products, preferred_element_type=jnp.float32)  2.63 us
    gather x2, local copies, waits for them, and re-layouts, column_tables(): outer = [jnp.take(jnp.asarray(v), order, axis=0)[:, None, :] for v in block]  2.6 us

profile of v1, /device:TPU:0, one launch (start us, length us, event | category | flops | bytes accessed | tf_op | source)
XLA Modules:
  0.0 128.9 jit_solution(7361541576469227377)
XLA Ops:
  0.0 0.1 broadcast_add_fusion
  0.1 0.1 add.729
  0.2 1.3 %gather_fusion = f32[4,1024]{1,0:T(4,128)S(1)} fusion(f32[4,1024]{1,0:T(4,128)} %constant.190.clone2.1, s32[1024]{0:T(1024)S(1)} %pad_clamp_fusion), kind=kCustom, calls=%fused_computation.clone | custom fusion | bytes 32784 | tf_op jit(solution)/shard_map/jit(_take)/gather | solution.py:59
  1.5 1.3 %gather_fusion.1 = f32[4,1024]{1,0:T(4,128)S(1)} fusion(f32[4,1024]{1,0:T(4,128)} %constant.191.clone2.1, s32[1024]{0:T(1024)S(1)} %pad_clamp_fusion), kind=kCustom, calls=%fused_computation.1.clone | custom fusion | bytes 32784 | tf_op jit(solution)/shard_map/jit(_take)/gather | solution.py:59
  2.8 0.1 broadcast_select_fusion.1
  2.9 1.2 multiply_subtract_fusion
  4.1 0.0 copy-start.7
  4.1 0.0 copy-start.8
  4.1 2.5 %add_convert_fusion = (bf16[4,256,1024]{2,1,0:T(8,128)(2,1)}, bf16[4,256,1024]{2,1,0:T(8,128)(2,1)S(1)}) fusion(f32[256,1024]{1,0:T(8,128)S(1)} %bitcast.196, f32[4,1024]{1,0:T(4,128)S(1)} %get-tuple-element.36, f32[256,1024]{1,0:T(8,128)S(1)} %bitcast.195, f32[4,1024]{1,0:T(4,128)S(1)} %get-tuple-element.35), kind=kLoop, calls=%fused_computation.2 | loop fusion | flops 8388608 | bytes 6324224 | tf_op jit(solution)/shard_map/convert_element_type | solution.py:60
  6.6 0.1 fusion.33
  7.4 2.1 %subtract_divide_fusion = (f32[2,2,32,1024]{3,2,1,0:T(8,128)S(1)}, f32[2,2,32,1024]{3,2,1,0:T(8,128)S(1)}) fusion(f32[]{:T(128)} %bitcast.10, f32[1024]{0:T(1024)S(1)} %fusion.28, f32[2,2,32]{2,1,0:T(2,128)S(1)} %fusion.35), kind=kLoop, calls=%fused_computation.22 | loop fusion | flops 917504 | bytes 1053188 | tf_op jit(solution)/shard_map/div | solution.py:78
  9.6 0.0 copy-start
  9.6 0.0 copy-start.2
  10.4 0.1 copy.23.info
  10.5 0.0 copy-done.7
  10.5 0.0 copy-done.8
  10.6 1.2 convert_element_type.140
  11.7 0.2 fusion.3.keep
  11.9 0.2 fusion.4.send
  12.2 0.0 copy-start.4
  12.2 45.2 %spectral_to_grid.1 = bf16[2,8,64,384]{3,2,1,0:T(8,128)(2,1)S(1)} custom-call(bf16[2,3,2,32,256]{4,3,2,1,0:T(8,128)(2,1)S(1)} %fusion.3.keep, bf16[2,3,2,32,256]{4,3,2,1,0:T(8,128)(2,1)S(1)} %fusion.4.send, bf16[3,2,16,256]{3,2,1,0:T(8,128)(2,1)S(1)} %slice.60.edge, f32[2,2,32,1024]{3,2,1,0:T(8,128)S(1)} %get-tuple-element.13.sine, ...), custom_call_target="tpu_custom_call" | custom-call | tf_op jit(solution)/shard_map/spectral_to_grid/pallas_call | solution.py:444
  57.4 0.0 copy-done
  57.4 0.0 copy-done.2
  57.4 0.0 copy-done.4
  57.4 1.0 multiply_bitcast_fusion
  58.5 0.1 fusion.15
  58.6 0.1 fusion.17
  58.6 0.1 fusion.18
  58.7 2.6 %fusion = bf16[1024,640]{0,1:T(8,128)(2,1)} fusion(bf16[1024,640]{0,1:T(8,128)(2,1)S(1)} %fusion.18, bf16[1024,1024]{1,0:T(8,128)(2,1)S(1)} %copy-done.4), kind=kOutput, calls=%fused_computation.6 | convolution fusion | flops 1342832640 | bytes 4718592 | tf_op jit(solution)/shard_map/dot_general | solution.py:476
  61.3 1.7 %copy.24 = bf16[1024,640]{1,0:T(8,128)(2,1)S(1)} copy(bf16[1024,640]{0,1:T(8,128)(2,1)} %fusion) | data formatting | bytes 2621440 | tf_op jit(solution)/shard_map/convert_element_type | solution.py:476
  63.0 0.0 copy-start.1
  63.0 1.0 copy-done.1
  64.1 0.0 copy-start.3
  64.1 1.0 copy-done.3
  65.1 59.0 %grid_to_spectral.1 = (bf16[2,3,2,32,256]{4,3,2,1,0:T(8,128)(2,1)S(1)}, bf16[2,3,2,32,256]{4,3,2,1,0:T(8,128)(2,1)S(1)}, bf16[3,2,16,256]{3,2,1,0:T(8,128)(2,1)S(1)}) custom-call(bf16[2,8,64,640]{3,2,1,0:T(8,128)(2,1)S(1)} %bitcast.189, f32[2,2,32,1024]{3,2,1,0:T(8,128)S(1)} %copy-done.3, f32[2,2,32,1024]{3,2,1,0:T(8,128)S(1)} %copy-done.1, ...), custom_call_target="tpu_custom_call" | custom-call | tf_op jit(solution)/shard_map/grid_to_spectral/pallas_call | solution.py:479
  124.1 0.0 copy-start.5
  124.1 0.0 copy-start.6
  124.2 1.4 %copy.28 = f32[3,2,128,256]{2,3,1,0:T(8,128)S(1)} copy(f32[3,2,128,256]{3,2,1,0:T(8,128)} %param.16) | data formatting | bytes 1572864 | tf_op args[0]
  125.6 0.0 copy-done.5
  125.6 0.0 copy-done.6
  125.6 0.4 fusion.2
  126.1 0.8 multiply_add_fusion.8
  126.9 0.7 multiply_add_fusion.4
  127.7 0.1 pad_maximum_fusion
  127.7 1.1 copy.29
  (28 shorter events, 0.4 us)
Async XLA Ops:
  4.1 6.4 %copy-start.7 = (bf16[2,64,128]{2,1,0:T(8,128)(2,1)S(1)}, bf16[2,64,128]{2,1,0:T(8,128)(2,1)}, u32[]{:S(2)}) copy-start(bf16[2,64,128]{2,1,0:T(8,128)(2,1)} %constant.387) | copy-start | bytes 98308
  4.1 6.4 %copy-start.8 = (bf16[2,64,128]{2,1,0:T(8,128)(2,1)S(1)}, bf16[2,64,128]{2,1,0:T(8,128)(2,1)}, u32[]{:S(2)}) copy-start(bf16[2,64,128]{2,1,0:T(8,128)(2,1)} %constant.388) | copy-start | bytes 98308
  9.6 47.8 %copy-start = (f32[2,2,32,1024]{3,2,1,0:T(8,128)}, f32[2,2,32,1024]{3,2,1,0:T(8,128)S(1)}, u32[]{:S(2)}) copy-start(f32[2,2,32,1024]{3,2,1,0:T(8,128)S(1)} %get-tuple-element.14.cosine) | copy-start | bytes 1572868
  9.6 47.8 %copy-start.2 = (f32[2,2,32,1024]{3,2,1,0:T(8,128)}, f32[2,2,32,1024]{3,2,1,0:T(8,128)S(1)}, u32[]{:S(2)}) copy-start(f32[2,2,32,1024]{3,2,1,0:T(8,128)S(1)} %get-tuple-element.13.sine) | copy-start | bytes 1572868
  12.2 45.2 %copy-start.4 = (bf16[1024,1024]{1,0:T(8,128)(2,1)S(1)}, bf16[1024,1024]{1,0:T(8,128)(2,1)}, u32[]{:S(2)}) copy-start(bf16[1024,1024]{1,0:T(8,128)(2,1)} %constant.192.clone) | copy-start | bytes 6291460
  63.0 1.0 copy-start.1
  64.1 1.0 copy-start.3
  124.1 1.5 %copy-start.5 = (bf16[128,144]{0,1:T(8,128)(2,1)S(1)}, bf16[128,144]{0,1:T(8,128)(2,1)}, u32[]{:S(2)}) copy-start(bf16[128,144]{0,1:T(8,128)(2,1)} %constant.389) | copy-start | bytes 110596
  124.1 1.5 %copy-start.6 = (bf16[128,144]{0,1:T(8,128)(2,1)S(1)}, bf16[128,144]{0,1:T(8,128)(2,1)}, u32[]{:S(2)}) copy-start(bf16[128,144]{0,1:T(8,128)(2,1)} %constant.390) | copy-start | bytes 110596

commit v2 on v1

v2 whole, which is shorter than its diff:
```python
import functools

import jax
import jax.numpy as jnp
import ml_dtypes
import numpy as np
from jax import lax
from jax.experimental import pallas as pl
from jax.experimental.pallas import tpu as pltpu
from jax.sharding import PartitionSpec as P

coriolis = 1.0
wave_speed = 6.0
phase_step = 0.25
time_step = 2.0
weight_scale = 4.0


def wave_of(positions, length):
    shifted = (positions + length // 2) % length - length // 2
    return shifted.astype(jnp.float32) * (2.0 / length)


def circle(products, length):
    angles = (products % length) * (2.0 * np.pi / length)
    return np.cos(angles).astype(np.float32), np.sin(angles).astype(np.float32)


def slot_base(slot, slots, half):
    return np.where(slot < slots // 2, 2 * half * slot, 2 * half * (slots - 1 - slot) + half)


def packed_table(length, slots, chunks):
    half = length // (2 * slots)
    rows = slot_base(np.arange(slots), slots, half)[:, None] + np.arange(half)
    cosine, sine = circle(rows[:, :, None] * np.arange(length), length)
    packed = np.stack([cosine, -sine], axis=1)
    packed[0, 1, 0] = circle(length // 2 * np.arange(length), length)[0]
    packed = packed.reshape(slots, 2, chunks, half // chunks, length).transpose(2, 0, 1, 3, 4)
    return packed.reshape(length, length).astype(ml_dtypes.bfloat16)


def turned(first, second):
    (c, s), (d, t) = first, second
    return c * d - s * t, s * d + c * t


def angle_tables(length, width, owners):
    y = np.arange(length)
    return [
        jnp.asarray(np.stack(circle(step * np.arange(count)[:, None] * y, length)))
        for step, count in ((width, owners), (FINE, width // FINE), (1, FINE))
    ]


def wave_operator(fields, kx, ky):
    (er, ei), (nr, ni), (hr, hi) = fields
    cx, cy = wave_speed * kx, wave_speed * ky
    return (
        (coriolis * nr + cx * hi, coriolis * ni - cx * hr),
        (cy * hi - coriolis * er, -coriolis * ei - cy * hr),
        (cx * ei + cy * ni, -(cx * er + cy * nr)),
    )


def wave_factors(kx, ky, phase):
    square = coriolis * coriolis + wave_speed * wave_speed * (kx * kx + ky * ky)
    frequency = jnp.sqrt(square)
    angle = frequency * phase
    return jnp.sin(angle) / frequency, (1.0 - jnp.cos(angle)) / square


def wave_exponential(fields, kx, ky, factors):
    sine, cosine = factors
    single = wave_operator(fields, kx, ky)
    double = wave_operator(single, kx, ky)
    return tuple(
        tuple(w + sine * a + cosine * b for w, a, b in zip(ws, one, two))
        for ws, one, two in zip(fields, single, double)
    )


def planes(fields):
    return tuple((fields[i, 0], fields[i, 1]) for i in range(fields.shape[0]))


MESH = pl.DeviceIdType.MESH
EDGE = 16
FINE = 16


def column(info, t, index):
    return info[t, :, index : index + 1]


def positions():
    g, a = lax.axis_index("space"), lax.axis_index("avg")
    return g, a, a // 2, a % 2


def edge_partner(g, slots):
    aligned = 1 - (g % (slots // 2) + slots // 2 - 1) // (slots // 2)
    return ((slots - g) % slots + aligned * (slots // 2)) % slots


def greet(slots, chips, edges):
    g, a, q, core = positions()
    barrier = pltpu.get_barrier_semaphore()
    peers = [((g + d) % slots, a) for d in range(1, slots)]
    peers += [(g, 2 * q + 1 - core)]
    peers += [(g, 2 * ((q + m) % chips) + core) for m in range(1, chips)]
    if edges:
        across = edge_partner(g, slots)
        peers += [
            (across, 2 * ((q + m) % chips) + (core + c) % 2)
            for c in range(2) for m in range(chips) if c or m
        ]
    for space, avg in peers:
        pl.semaphore_signal(
            barrier, inc=1, device_id={"space": space, "avg": avg}, device_id_type=MESH
        )
    pl.semaphore_wait(barrier, len(peers))


def remote(src, dst, send, recv, space, avg):
    return pltpu.make_async_remote_copy(
        src_ref=src, dst_ref=dst, send_sem=send, recv_sem=recv,
        device_id={"space": space, "avg": avg}, device_id_type=MESH,
    )


DIMS_NT = (((1,), (1,)), ((), ()))


def step_kernel(
    dims, state, into_rows, back_rows, info, ky, own_kx, phase, blocks, steps, fines, packed_hbm, result,
    moved, top, gx, eg, rows_c, rows_s, half, arr, arr_t, grid, products, packed, ct, st, sine, cosine,
    end_sine, end_cosine, fh, ret, lhs, stage, rsin, acc, xs, rx, fin, own, other, edge,
    ex_s, ex_r, eg_s, eg_r, x_s, x_r, c_s, c_r, a_s, a_r, l_s,
    b_s, b_r, m_s, d_s, d_r, y_s, y_r, gv_s, gv_r, le_s, le_r, bring_s,
):
    slots, chips, chunks, hb, width, block = dims
    length, reach = slots * block, block // 2
    g, a, q, core = positions()
    low, high = g < slots // 2, g >= slots // 2
    partner = 2 * q + 1 - core
    across = edge_partner(g, slots)
    bring = pltpu.make_async_copy(packed_hbm, packed, bring_s)

    for f in range(3):
        for i in range(2):
            plane = state[f, i].astype(jnp.bfloat16)
            top[f, i] = plane[:EDGE]
            picked = jnp.dot(into_rows[...], plane, preferred_element_type=jnp.float32)
            picked = picked.astype(jnp.bfloat16)
            for s in range(2):
                for t in range(chunks):
                    spot = s * reach + t * hb
                    moved[s, t, f, i] = picked[spot : spot + hb]
    greet(slots, chips, True)

    def build_factors(unused):
        for t in range(chunks):
            for s in range(2):
                def one(j, carry, t=t, s=s):
                    span = pl.ds(pl.multiple_of(j * 256, 256), 256)
                    factors = wave_factors(column(info, t, s), ky[:, span], phase[...])
                    sine[t, s, :, span], cosine[t, s, :, span] = factors
                    return carry
                lax.fori_loop(0, length // 256, one, 0)

    def own_factors():
        end_sine[...], end_cosine[...] = wave_factors(own_kx[...], ky[:, :width], time_step)

    def build_tables():
        for c in range(2):
            for m in range(chips):
                owner = 2 * ((q + m) % chips) + (core + c) % 2
                first = (blocks[0, pl.ds(owner, 1), :], blocks[1, pl.ds(owner, 1), :])

                def one(h, carry, j=c * chips + m, first=first):
                    begin = turned(first, (steps[0, pl.ds(h, 1), :], steps[1, pl.ds(h, 1), :]))
                    cos_rows, sin_rows = turned(begin, (fines[0], fines[1]))
                    at = pl.ds(pl.multiple_of(j * width + h * FINE, FINE), FINE)
                    ct[at, :] = cos_rows.astype(jnp.bfloat16)
                    st[at, :] = sin_rows.astype(jnp.bfloat16)
                    return carry
                lax.fori_loop(0, width // FINE, one, 0)

    exchange = [
        remote(moved.at[1, t], gx.at[t, 1, 0, 0], ex_s.at[t], ex_r.at[t], slots - 1 - g, a)
        for t in range(chunks)
    ]
    edges = [
        remote(top, eg.at[c, m], eg_s.at[c, m], eg_r.at[c, m],
               across, 2 * ((q + chips - m) % chips) + (core + c) % 2)
        for c in range(2) for m in range(chips)
    ]

    def mine(t, s):
        return gx.at[t, 1, 0, 0] if s else moved.at[0, t]

    def over_chips(t, s, m):
        return remote(mine(t, s), gx.at[t, s, 0, m], x_s.at[t, s, m], x_r.at[t, s, m],
                      g, 2 * ((q + chips - m) % chips) + core)

    def over_cores(t, s, m):
        source = gx.at[t, s, 0, m] if m else mine(t, s)
        return remote(source, gx.at[t, s, 1, m], c_s.at[t, s, m], c_r.at[t, s, m], g, partner)

    def to_grid(t, d):
        to = (g + d) % slots
        return remote(half.at[t, to], arr.at[t, g], a_s.at[t, d], a_r.at[t, d], to, a)

    exchange[0].start()

    @pl.when(high)
    def _():
        for copy in edges:
            copy.start()
        eg[...] = jnp.zeros_like(eg)

    for t in range(1, chunks):
        exchange[t].start()
    for t in range(chunks):
        for m in range(1, chips):
            over_chips(t, 0, m).start()
        over_cores(t, 0, 0).start()
    bring.start()
    build_factors(0)
    build_tables()
    for t in range(chunks):
        for m in range(1, chips):
            over_chips(t, 0, m).wait_recv()
            over_cores(t, 0, m).start()
    for t in range(chunks):
        exchange[t].wait_recv()
        for m in range(1, chips):
            over_chips(t, 1, m).start()
        over_cores(t, 1, 0).start()
        for m in range(1, chips):
            over_chips(t, 1, m).wait_recv()
            over_cores(t, 1, m).start()
        if t == 0:
            @pl.when(low)
            def _():
                for copy in edges:
                    copy.wait_recv()
        for s in range(2):
            for m in range(chips):
                over_cores(t, s, m).wait_recv()
        own_pair = column(info, t, 2) > 0.5
        sign = column(info, t, 3)
        for j in range(2 * chips):
            c, m = divmod(j, chips)
            span = slice(j * width, (j + 1) * width)
            turned_rows = []
            for s in range(2):
                source = moved.at[0, t] if s + j == 0 else gx.at[t, s, c, m]
                fields = [[source[f, i].astype(jnp.float32) for i in range(2)] for f in range(3)]
                if s == 1 and t == 0:
                    put = column(info, t, 4)[:EDGE] > 0.5
                    for f in range(3):
                        for i in range(2):
                            top = jnp.where(put, eg[c, m, f, i].astype(jnp.float32), fields[f][i][:EDGE])
                            fields[f][i] = (
                                jnp.concatenate([top, fields[f][i][EDGE:]], axis=0) if hb > EDGE else top
                            )
                turned_rows.append(wave_exponential(
                    fields, column(info, t, s), ky[:, span], (sine[t, s, :, span], cosine[t, s, :, span])
                ))
            for f in range(3):
                (re0, im0), (re1, im1) = turned_rows[0][f], turned_rows[1][f]
                for i, value in enumerate((
                    jnp.where(own_pair, re0, re0 + re1), jnp.where(own_pair, re1, sign * (im0 - im1))
                )):
                    rows_c[(i * 3 + f) * hb : (i * 3 + f + 1) * hb, span] = value.astype(jnp.bfloat16)
                for i, value in enumerate((
                    jnp.where(own_pair, -im0, -(im0 + im1)), jnp.where(own_pair, -im1, sign * (re0 - re1))
                )):
                    rows_s[(i * 3 + f) * hb : (i * 3 + f + 1) * hb, span] = value.astype(jnp.bfloat16)
        tile = min(length, max(block, 256))
        for y in range(0, length, tile):
            value = (
                jnp.dot(rows_c[...], ct[:, y : y + tile], preferred_element_type=jnp.float32)
                + jnp.dot(rows_s[...], st[:, y : y + tile], preferred_element_type=jnp.float32)
            ).astype(jnp.bfloat16)
            for b in range(tile // block):
                for i in range(2):
                    for f in range(3):
                        half[t, y // block + b, i * hb : (i + 1) * hb, f * block : (f + 1) * block] = (
                            value[(i * 3 + f) * hb : (i * 3 + f + 1) * hb, b * block : (b + 1) * block]
                        )
        for d in range(1, slots):
            to_grid(t, d).start()
        pltpu.make_async_copy(half.at[t, g], arr.at[t, g], l_s.at[t]).start()
    def to_rows(t, d):
        to = (g + d) % slots
        return remote(fh.at[t, to], ret.at[t, g], b_s.at[t, d], b_r.at[t, d], to, a)

    def sum_cores(t):
        return remote(stage.at[t, 1], rsin.at[t], d_s.at[t], d_r.at[t], g, partner)

    def sum_chips(t, m):
        return remote(xs.at[t, m], rx.at[t, m], y_s.at[t, m], y_r.at[t, m],
                      g, 2 * ((q + m) % chips) + core)

    def give(t):
        return remote(fin.at[t], other.at[t], gv_s.at[t], gv_r.at[t], slots - 1 - g, a)

    last = remote(fin.at[0, :, :, :EDGE], edge, le_s, le_r, edge_partner(g, slots), a)

    bring.wait()
    for t in range(chunks):
        for d in range(1, slots):
            to_grid(t, d).wait_recv()
        pltpu.make_async_copy(half.at[t, g], arr.at[t, g], l_s.at[t]).wait()
        together = max(1, 128 // (2 * hb))
        for p in range(0, slots, together):
            value = arr[t, p : p + together].astype(jnp.float32)
            value = value.reshape(together * 2 * hb, 3 * block)
            spot = p * 2 * hb
            arr_t[:, spot : spot + together * 2 * hb] = value.T.astype(jnp.bfloat16)
        depth = length // chunks
        for x in range(0, length, 256):
            value = jnp.dot(
                arr_t[...], packed[t * depth : (t + 1) * depth, x : x + 256],
                preferred_element_type=jnp.float32,
            )
            if t:
                value = value + grid[:, x : x + 256]
            if t < chunks - 1:
                grid[:, x : x + 256] = value
            else:
                value = value * (1.0 / length)
                east, north, height = (value[i * block : (i + 1) * block] for i in range(3))
                for k, pair in enumerate((
                    east * east, east * north, north * north, east * height, north * height
                )):
                    products[k * block : (k + 1) * block, x : x + 256] = pair.astype(jnp.bfloat16)
    for t in range(chunks):
        for k in range(0, depth, 256):
            value = lax.dot_general(
                packed[t * depth + k : t * depth + k + 256, :], products[...], DIMS_NT,
                preferred_element_type=jnp.float32,
            ).astype(jnp.bfloat16)
            for n in range(256 // (2 * hb)):
                fh[t, k // (2 * hb) + n] = value[n * 2 * hb : (n + 1) * 2 * hb]
        for d in range(1, slots):
            to_rows(t, d).start()
        pltpu.make_async_copy(fh.at[t, g], ret.at[t, g], m_s.at[t]).start()
    own_factors()

    @pl.when(low)
    def _():
        edge[...] = jnp.zeros_like(edge)

    for t in range(chunks):
        for d in range(1, slots):
            to_rows(t, d).wait_recv()
        pltpu.make_async_copy(fh.at[t, g], ret.at[t, g], m_s.at[t]).wait()
        for p in range(slots):
            for k in range(5):
                lhs[k * 2 * hb : (k + 1) * 2 * hb, p * block : (p + 1) * block] = (
                    ret[t, p, :, k * block : (k + 1) * block]
                )
        own_pair = column(info, t, 2) > 0.5
        sign, scale = column(info, t, 3), column(info, t, 5)
        for j in range(2 * chips):
            c, m = divmod(j, chips)
            span = slice(j * width, (j + 1) * width)
            by_c = lax.dot_general(lhs[...], ct[span, :], DIMS_NT, preferred_element_type=jnp.float32)
            by_s = lax.dot_general(lhs[...], st[span, :], DIMS_NT, preferred_element_type=jnp.float32)

            def part(values, k, i):
                return values[(2 * k + i) * hb : (2 * k + i + 1) * hb]

            for s in range(2):
                turn = scale * sign if s == 0 else -scale * sign
                real, imag = [], []
                for k in range(5):
                    rc, ic = part(by_c, k, 0), part(by_c, k, 1)
                    rs, iz = part(by_s, k, 0), part(by_s, k, 1)
                    real.append(jnp.where(own_pair, scale * (ic if s else rc), scale * rc + turn * iz))
                    imag.append(jnp.where(own_pair, -scale * (iz if s else rs), turn * ic - scale * rs))
                kx, kyj = column(info, t, s), ky[:, span]
                tendency = [
                    (kx * imag[u] + kyj * imag[v], -(kx * real[u] + kyj * real[v]))
                    for u, v in ((0, 1), (1, 2), (3, 4))
                ]
                back = wave_exponential(
                    tendency, kx, kyj, (-sine[t, s, :, span], cosine[t, s, :, span])
                )
                for f in range(3):
                    for i in range(2):
                        stage[t, c, m, s, f, i] = back[f][i].astype(jnp.bfloat16)
        sum_cores(t).start()
        sum_cores(t).wait_recv()
        for m in range(1, chips):
            xs[t, m] = (
                stage[t, 0, m].astype(jnp.float32) + rsin[t, m].astype(jnp.float32)
            ).astype(jnp.bfloat16)
            sum_chips(t, m).start()
        acc[...] = stage[t, 0, 0].astype(jnp.float32) + rsin[t, 0].astype(jnp.float32)
        for m in range(1, chips):
            sum_chips(t, m).wait_recv()
            acc[...] += rx[t, m].astype(jnp.float32)
        fin[t] = acc[1].astype(jnp.bfloat16)
        give(t).start()
        if t == 0:
            @pl.when(low)
            def _():
                last.start()
        own[t] = acc[0].astype(jnp.bfloat16)
    for t in range(chunks):
        give(t).wait_recv()

    @pl.when(high)
    def _():
        last.wait_recv()

    for t in range(chunks):
        exchange[t].wait_send()
        for s in range(2):
            for m in range(1, chips):
                over_chips(t, s, m).wait_send()
            for m in range(chips):
                over_cores(t, s, m).wait_send()
        for d in range(1, slots):
            to_grid(t, d).wait_send()

    @pl.when(high)
    def _():
        for copy in edges:
            copy.wait_send()


    for t in range(chunks):
        for d in range(1, slots):
            to_rows(t, d).wait_send()
        sum_cores(t).wait_send()
        for m in range(1, chips):
            sum_chips(t, m).wait_send()
        give(t).wait_send()

    @pl.when(low)
    def _():
        last.wait_send()


    for f in range(3):
        for i in range(2):
            rows = jnp.concatenate(
                [own[t, f, i] for t in range(chunks)] + [other[t, f, i] for t in range(chunks)]
                + [edge[f, i]], axis=0,
            )
            averaged = jnp.dot(back_rows[...], rows, preferred_element_type=jnp.float32)
            result[f, i] = state[f, i] + time_step * averaged
    fields = [[result[f, i] for i in range(2)] for f in range(3)]
    advanced = wave_exponential(fields, own_kx[...], ky[:, :width], (end_sine[...], end_cosine[...]))
    for f in range(3):
        for i in range(2):
            result[f, i] = advanced[f][i]


VMEM = pl.BlockSpec(memory_space=pltpu.VMEM)


def per_device(spectral_state, phase_index, weight_count):
    slots, owners = lax.axis_size("space"), lax.axis_size("avg")
    block, width = spectral_state.shape[2:]
    length, half = block * slots, block // 2
    chips = owners // 2
    chunks = max(1, half // CHUNK_ROWS)
    hb = half // chunks
    dims = (slots, chips, chunks, hb, width, block)
    g, a = lax.axis_index("space"), lax.axis_index("avg")
    q, core = a // 2, a % 2
    low = g < slots // 2
    phase = phase_index[0].astype(jnp.float32) * phase_step
    weight = weight_count[0].astype(jnp.float32) / (weight_scale * owners)

    m, c = jnp.arange(chips, dtype=jnp.int32), jnp.arange(2, dtype=jnp.int32)[:, None]
    order = (2 * ((q + m) % chips) + (core + c) % 2).reshape(-1)
    columns = (order[:, None] * width + jnp.arange(width, dtype=jnp.int32)).reshape(1, -1)
    ky = wave_of(columns, length)
    packed = jnp.asarray(packed_table(length, slots, chunks))

    base = jnp.where(low, 2 * half * g, 2 * half * (slots - 1 - g) + half)
    direct = base + jnp.arange(half, dtype=jnp.int32)
    mirror = jnp.where(direct == 0, length // 2, length - direct)
    first = wave_of(jnp.where(low, direct, mirror), length)
    second = wave_of(jnp.where(low, mirror, direct), length)
    ones = jnp.ones((half,), jnp.float32)
    start = (jnp.arange(half) == 0) & low
    info = jnp.stack([
        first, second, (direct == 0).astype(jnp.float32), jnp.where(low, ones, -ones),
        start.astype(jnp.float32), ones * (weight / length), ones, ones,
    ], axis=1).reshape(chunks, hb, 8)
    own_kx = wave_of(g * block + jnp.arange(block, dtype=jnp.int32)[:, None], length)

    r = np.arange(half)
    into = np.zeros((2, 2, half, block), np.float32)
    into[0, 0, r, r] = 1
    into[0, 1, r, half + r] = 1
    into[1, 0, r, half - r] = 1
    into[1, 1, r[1:], block - r[1:]] = 1
    into = jnp.asarray(into.reshape(2, block, block).astype(ml_dtypes.bfloat16))
    into = jnp.where(low, into[0], into[1])
    back = np.zeros((2, block, 2 * half + EDGE), np.float32)
    back[0, r, r] = 1
    back[0, half + r, half + r] = 1
    back[1, half - r, r] = 1
    back[1, block - r[1:], half + r[1:]] = 1
    back[1, 0, 2 * half] = 1
    back = jnp.asarray(back.astype(ml_dtypes.bfloat16))
    back = jnp.where(low, back[0], back[1])

    piece = (3, 2, hb, width)
    dma = pltpu.SemaphoreType.DMA
    vmem = lambda *shape: pltpu.VMEM(shape, jnp.bfloat16)
    wide = lambda *shape: pltpu.VMEM(shape, jnp.float32)
    return pl.pallas_call(
        functools.partial(step_kernel, dims),
        out_shape=jax.ShapeDtypeStruct(spectral_state.shape, jnp.float32),
        in_specs=[VMEM] * 10 + [pl.BlockSpec(memory_space=pl.ANY)],
        out_specs=VMEM,
        scratch_shapes=[
            vmem(2, chunks, *piece), vmem(3, 2, EDGE, width),
            vmem(chunks, 2, 2, chips, *piece), vmem(2, chips, 3, 2, EDGE, width),
            vmem(6 * hb, length), vmem(6 * hb, length),
            vmem(chunks, slots, 2 * hb, 3 * block), vmem(chunks, slots, 2 * hb, 3 * block),
            vmem(3 * block, length // chunks), wide(3 * block, length), vmem(5 * block, length),
            vmem(length, length), vmem(length, length), vmem(length, length),
            wide(chunks, 2, hb, length), wide(chunks, 2, hb, length),
            wide(block, width), wide(block, width),
            vmem(chunks, slots, 2 * hb, 5 * block), vmem(chunks, slots, 2 * hb, 5 * block),
            vmem(10 * hb, length),
            vmem(chunks, 2, chips, 2, *piece), vmem(chunks, chips, 2, *piece),
            wide(2, *piece), vmem(chunks, chips, 2, *piece), vmem(chunks, chips, 2, *piece),
            vmem(chunks, *piece), vmem(chunks, *piece), vmem(chunks, *piece),
            vmem(3, 2, EDGE, width),
            dma((chunks,)), dma((chunks,)),
            dma((2, chips)), dma((2, chips)),
            dma((chunks, 2, chips)), dma((chunks, 2, chips)),
            dma((chunks, 2, chips)), dma((chunks, 2, chips)),
            dma((chunks, slots)), dma((chunks, slots)), dma((chunks,)),
            dma((chunks, slots)), dma((chunks, slots)), dma((chunks,)),
            dma((chunks,)), dma((chunks,)),
            dma((chunks, chips)), dma((chunks, chips)),
            dma((chunks,)), dma((chunks,)),
            dma(()), dma(()), dma(()),
        ],
        compiler_params=pltpu.CompilerParams(
            collective_id=0, has_side_effects=True, vmem_limit_bytes=56 * 2**20
        ),
        name="averaged_step",
    )(spectral_state, into, back, info, ky, own_kx, phase.reshape(1, 1),
      *angle_tables(length, width, owners), packed)


CHUNK_ROWS = 32


def solution(mesh):
    in_specs = (P(None, None, "space", "avg"), P("avg"), P("avg"))
    out_specs = P(None, None, "space", "avg")
    return jax.shard_map(
        per_device, mesh=mesh, in_specs=in_specs, out_specs=out_specs, check_vma=False
    )
```

time: 129 us -> 112 us (0.87)
  local copies, waits for them, and re-layouts: 9.21 us -> 2.92 us
  other arithmetic: 9.3 us -> 4.33 us
  matrix products: 4.46 us -> 0 us
    dot_general x5 -> x0, matrix products: 4.46 us -> none  [the longest x1 2.63 us: per_device(): jnp.dot(packed, products, preferred_element_type=jnp.float32)]
    convert_element_type x3 -> x0, other arithmetic: 3.67 us -> none  [the longest x1 2.49 us: column_tables(): v.reshape(groups * width, length).astype(jnp.bfloat16)]
    select_n x2, other arithmetic: 0.08 us -> 2.86 us  [the longest x1 1.48 us: per_device(): back = jnp.where(low, back[0], back[1])]
    gather x2 -> x0, local copies, waits for them, and re-layouts: 2.6 us -> none  [column_tables(): outer = [jnp.take(jnp.asarray(v), order, axis=0)[:, None, :] for v in block]]
    div x1 -> x0, other arithmetic: 2.15 us -> none  [wave_factors(): return (jnp.sin(angle) / frequency, (1.0 - jnp.cos(angle)) / square)]
    convert_element_type x1 -> x0, local copies, waits for them, and re-layouts: 1.7 us -> none  [per_device(): jnp.dot(packed, products, preferred_element_type=jnp.float32)]
    add x3 -> x0, other arithmetic: 1.6 us -> none  [the longest x2 1.53 us: wave_exponential(): w + sine * a + cosine * b]
    unnamed x21 -> x2, local copies, waits for them, and re-layouts: 3.52 us -> 2.11 us
where the time goes in v2:
time: 112 us
  Pallas kernels  103 us (92%)
  other arithmetic  4.33 us (4%)
  local copies, waits for them, and re-layouts  2.92 us (3%)
  between operations  1.34 us (1%)
    pallas_call x1, Pallas kernels, per_device(): pl.pallas_call(functools.partial(step_kernel, dims), out_shape=jax.ShapeD...  103 us

profile of v2, /device:TPU:0, one launch (start us, length us, event | category | flops | bytes accessed | tf_op | source)
XLA Modules:
  0.0 111.9 jit_solution(969538985286416578)
XLA Ops:
  1.3 0.1 add_multiply_fusion
  1.4 0.1 mul.70
  1.6 0.1 add_bitcast_fusion
  1.6 0.6 fusion.6.ky
  2.2 0.7 copy.12.info
  2.9 1.4 %select_bitcast_fusion.1.into_rows = bf16[128,128]{1,0:T(8,128)(2,1)} fusion(bf16[1,128,128]{2,1,0:T(8,128)(2,1)} %constant.150, bf16[1,128,128]{2,1,0:T(8,128)(2,1)} %constant.151, pred[]{:T(512)S(6)} %lt.43), kind=kLoop, calls=%fused_computation.8 | loop fusion | flops 16384 | bytes 98305 | tf_op jit(solution)/shard_map/jit(_where)/select_n | solution.py:509
  4.3 1.5 %select_bitcast_fusion.back_rows = bf16[128,144]{1,0:T(8,128)(2,1)} fusion(bf16[1,128,144]{2,1,0:T(8,128)(2,1)} %constant.152, bf16[1,128,144]{2,1,0:T(8,128)(2,1)} %constant.153, pred[]{:T(512)S(6)} %lt.43), kind=kLoop, calls=%fused_computation.7 | loop fusion | flops 18432 | bytes 110593 | tf_op jit(solution)/shard_map/jit(_where)/select_n | solution.py:517
  5.8 0.7 fusion.3.own_kx
  6.5 103.3 %averaged_step.1 = f32[3,2,128,256]{3,2,1,0:T(8,128)} custom-call(f32[3,2,128,256]{3,2,1,0:T(8,128)} %state.1, bf16[128,128]{1,0:T(8,128)(2,1)} %select_bitcast_fusion.1.into_rows, bf16[128,144]{1,0:T(8,128)(2,1)} %select_bitcast_fusion.back_rows, f32[2,32,8]{2,1,0:T(8,128)} %copy.12.info, f32[1,1024]{1,0:T(1,128)} %fusion.6.ky, f32[128,1]{1,0:T(8,128)} %fusion.3.own_kx, ...), custom_call_target="tpu_custom_call" | custom-call | tf_op jit(solution)/shard_map/averaged_step/pallas_call | solution.py:523
  109.8 2.1 %copy.17 = f32[3,2,128,256]{3,2,1,0:T(8,128)} copy(f32[3,2,128,256]{3,2,1,0:T(8,128)} %averaged_step.1) | data formatting | bytes 1572864
  (8 shorter events, 0.1 us)

commit v3 on v2

--- a/solution.py
+++ b/solution.py
@@ -122,6 +122,10 @@
     pl.semaphore_wait(barrier, len(peers))
 
 
+def sending(slots):
+    return sorted(range(1, slots), key=lambda d: (-min(d, slots - d), d))
+
+
 def remote(src, dst, send, recv, space, avg):
     return pltpu.make_async_remote_copy(
         src_ref=src, dst_ref=dst, send_sem=send, recv_sem=recv,
@@ -145,13 +149,14 @@
     low, high = g < slots // 2, g >= slots // 2
     partner = 2 * q + 1 - core
     across = edge_partner(g, slots)
+    side = g // (slots // 2)
     bring = pltpu.make_async_copy(packed_hbm, packed, bring_s)
 
     for f in range(3):
         for i in range(2):
             plane = state[f, i].astype(jnp.bfloat16)
             top[f, i] = plane[:EDGE]
-            picked = jnp.dot(into_rows[...], plane, preferred_element_type=jnp.float32)
+            picked = jnp.dot(into_rows[side], plane, preferred_element_type=jnp.float32)
             picked = picked.astype(jnp.bfloat16)
             for s in range(2):
                 for t in range(chunks):
@@ -291,7 +296,7 @@
                         half[t, y // block + b, i * hb : (i + 1) * hb, f * block : (f + 1) * block] = (
                             value[(i * 3 + f) * hb : (i * 3 + f + 1) * hb, b * block : (b + 1) * block]
                         )
-        for d in range(1, slots):
+        for d in sending(slots):
             to_grid(t, d).start()
         pltpu.make_async_copy(half.at[t, g], arr.at[t, g], l_s.at[t]).start()
     def to_rows(t, d):
@@ -346,7 +351,7 @@
             ).astype(jnp.bfloat16)
             for n in range(256 // (2 * hb)):
                 fh[t, k // (2 * hb) + n] = value[n * 2 * hb : (n + 1) * 2 * hb]
-        for d in range(1, slots):
+        for d in sending(slots):
             to_rows(t, d).start()
         pltpu.make_async_copy(fh.at[t, g], ret.at[t, g], m_s.at[t]).start()
     own_factors()
@@ -454,7 +459,7 @@
                 [own[t, f, i] for t in range(chunks)] + [other[t, f, i] for t in range(chunks)]
                 + [edge[f, i]], axis=0,
             )
-            averaged = jnp.dot(back_rows[...], rows, preferred_element_type=jnp.float32)
+            averaged = jnp.dot(back_rows[side], rows, preferred_element_type=jnp.float32)
             result[f, i] = state[f, i] + time_step * averaged
     fields = [[result[f, i] for i in range(2)] for f in range(3)]
     advanced = wave_exponential(fields, own_kx[...], ky[:, :width], (end_sine[...], end_cosine[...]))
@@ -506,7 +511,6 @@
     into[1, 0, r, half - r] = 1
     into[1, 1, r[1:], block - r[1:]] = 1
     into = jnp.asarray(into.reshape(2, block, block).astype(ml_dtypes.bfloat16))
-    into = jnp.where(low, into[0], into[1])
     back = np.zeros((2, block, 2 * half + EDGE), np.float32)
     back[0, r, r] = 1
     back[0, half + r, half + r] = 1
@@ -514,7 +518,6 @@
     back[1, block - r[1:], half + r[1:]] = 1
     back[1, 0, 2 * half] = 1
     back = jnp.asarray(back.astype(ml_dtypes.bfloat16))
-    back = jnp.where(low, back[0], back[1])
 
     piece = (3, 2, hb, width)
     dma = pltpu.SemaphoreType.DMA
@@ -559,7 +562,7 @@
       *angle_tables(length, width, owners), packed)
 
 
-CHUNK_ROWS = 32
+CHUNK_ROWS = 16
 
 
 def solution(mesh):

time: 112 us -> 104 us (0.929)
  Pallas kernels: 103 us -> 97.8 us
  other arithmetic: 4.33 us -> 1.51 us
    pallas_call x1, Pallas kernels: 103 us -> 97.8 us  [per_device(): pl.pallas_call(functools.partial(step_kernel, dims), out_shape=jax.ShapeD...]
    select_n x2 -> x0, other arithmetic: 2.86 us -> none  [the longest x1 1.48 us: per_device(): back = jnp.where(low, back[0], back[1])]
where the time goes in v3:
time: 104 us
  Pallas kernels  97.8 us (94%)
  local copies, waits for them, and re-layouts  2.93 us (3%)
  other arithmetic  1.51 us (1%)
  between operations  1.34 us (1%)
    pallas_call x1, Pallas kernels, per_device(): pl.pallas_call(functools.partial(step_kernel, dims), out_shape=jax.ShapeD...  97.8 us
    unnamed x2, local copies, waits for them, and re-layouts  2.11 us

profile of v3, /device:TPU:0, one launch (start us, length us, event | category | flops | bytes accessed | tf_op | source)
XLA Modules:
  0.0 103.6 jit_solution(9327372807084984205)
XLA Ops:
  1.3 0.1 add_multiply_fusion
  1.4 0.1 mul.70
  1.5 0.1 add_bitcast_fusion
  1.6 0.6 fusion.18.ky
  2.2 0.7 fusion.3.own_kx
  2.9 0.7 stack.19.info
  3.7 97.8 %averaged_step.1 = f32[3,2,128,256]{3,2,1,0:T(8,128)} custom-call(f32[3,2,128,256]{3,2,1,0:T(8,128)} %state.1, bf16[2,128,128]{2,1,0:T(8,128)(2,1)} %constant.143.clone.into_rows, bf16[2,128,144]{2,1,0:T(8,128)(2,1)} %constant.144.clone.back_rows, f32[4,16,8]{2,1,0:T(8,128)} %stack.19.info, f32[1,1024]{1,0:T(1,128)} %fusion.18.ky, f32[128,1]{1,0:T(8,128)} %fusion.3.own_kx, ...), custom_call_target="tpu_custom_call" | custom-call | tf_op jit(solution)/shard_map/averaged_step/pallas_call | solution.py:526
  101.5 2.1 %copy.17 = f32[3,2,128,256]{3,2,1,0:T(8,128)} copy(f32[3,2,128,256]{3,2,1,0:T(8,128)} %averaged_step.1) | data formatting | bytes 1572864
  (7 shorter events, 0.1 us)

commit v4 on v3

--- a/solution.py
+++ b/solution.py
@@ -238,14 +238,19 @@
         for m in range(1, chips):
             over_chips(t, 0, m).wait_recv()
             over_cores(t, 0, m).start()
-    for t in range(chunks):
+    def spread(t):
         exchange[t].wait_recv()
         for m in range(1, chips):
             over_chips(t, 1, m).start()
         over_cores(t, 1, 0).start()
+
+    spread(0)
+    for t in range(chunks):
         for m in range(1, chips):
             over_chips(t, 1, m).wait_recv()
             over_cores(t, 1, m).start()
+        if t + 1 < chunks:
+            spread(t + 1)
         if t == 0:
             @pl.when(low)
             def _():
@@ -360,6 +365,18 @@
     def _():
         edge[...] = jnp.zeros_like(edge)
 
+    def finish(t):
+        for m in range(1, chips):
+            sum_chips(t, m).wait_recv()
+            acc[...] += rx[t, m].astype(jnp.float32)
+        fin[t] = acc[1].astype(jnp.bfloat16)
+        give(t).start()
+        if t == 0:
+            @pl.when(low)
+            def _():
+                last.start()
+        own[t] = acc[0].astype(jnp.bfloat16)
+
     for t in range(chunks):
         for d in range(1, slots):
             to_rows(t, d).wait_recv()
@@ -400,6 +417,8 @@
                     for i in range(2):
                         stage[t, c, m, s, f, i] = back[f][i].astype(jnp.bfloat16)
         sum_cores(t).start()
+        if t:
+            finish(t - 1)
         sum_cores(t).wait_recv()
         for m in range(1, chips):
             xs[t, m] = (
@@ -407,16 +426,7 @@
             ).astype(jnp.bfloat16)
             sum_chips(t, m).start()
         acc[...] = stage[t, 0, 0].astype(jnp.float32) + rsin[t, 0].astype(jnp.float32)
-        for m in range(1, chips):
-            sum_chips(t, m).wait_recv()
-            acc[...] += rx[t, m].astype(jnp.float32)
-        fin[t] = acc[1].astype(jnp.bfloat16)
-        give(t).start()
-        if t == 0:
-            @pl.when(low)
-            def _():
-                last.start()
-        own[t] = acc[0].astype(jnp.bfloat16)
+    finish(chunks - 1)
     for t in range(chunks):
         give(t).wait_recv()
 

time: 104 us -> 100 us (0.962)
  Pallas kernels: 97.8 us -> 94.1 us
    pallas_call x1, Pallas kernels: 97.8 us -> 94.1 us  [per_device(): pl.pallas_call(functools.partial(step_kernel, dims), out_shape=jax.ShapeD...]
where the time goes in v4:
time: 100 us; the launch traced here: 99.8 us
  Pallas kernels  94.1 us (94%)
  local copies, waits for them, and re-layouts  2.93 us (3%)
  other arithmetic  1.51 us (2%)
  between operations  1.34 us (1%)
    pallas_call x1, Pallas kernels, per_device(): pl.pallas_call(functools.partial(step_kernel, dims), out_shape=jax.ShapeD...  94.1 us
    unnamed x2, local copies, waits for them, and re-layouts  2.11 us

profile of v4, /device:TPU:0, one launch (start us, length us, event | category | flops | bytes accessed | tf_op | source)
XLA Modules:
  0.0 99.8 jit_solution(10128792758084447918)
XLA Ops:
  1.3 0.1 add_multiply_fusion
  1.4 0.1 mul.70
  1.5 0.1 add_bitcast_fusion
  1.6 0.6 fusion.18.ky
  2.2 0.7 fusion.3.own_kx
  2.9 0.7 stack.19.info
  3.7 94.1 %averaged_step.1 = f32[3,2,128,256]{3,2,1,0:T(8,128)} custom-call(f32[3,2,128,256]{3,2,1,0:T(8,128)} %state.1, bf16[2,128,128]{2,1,0:T(8,128)(2,1)} %constant.143.clone.into_rows, bf16[2,128,144]{2,1,0:T(8,128)(2,1)} %constant.144.clone.back_rows, f32[4,16,8]{2,1,0:T(8,128)} %stack.19.info, f32[1,1024]{1,0:T(1,128)} %fusion.18.ky, f32[128,1]{1,0:T(8,128)} %fusion.3.own_kx, ...), custom_call_target="tpu_custom_call" | custom-call | tf_op jit(solution)/shard_map/averaged_step/pallas_call | solution.py:536
  97.7 2.1 %copy.17 = f32[3,2,128,256]{3,2,1,0:T(8,128)} copy(f32[3,2,128,256]{3,2,1,0:T(8,128)} %averaged_step.1) | data formatting | bytes 1572864
  (7 shorter events, 0.1 us)
